TPU v7x, 256 devices: a whole 4x4x8 slice. The times are simulated.
256 devices in a mesh: leaf: 128 (over y, x, z), col: 2 (over core).
Axes of the slice: x: 4, y: 4, z: 8, core: 2. Of those that a mesh axis runs over, the one named last changes fastest.
Arguments:
- sources: bfloat16 [524288, 256], P('leaf', 'col'), may hold values from -6 to 6
- near_tiles: bfloat16 [2048, 8, 256, 256], P('leaf', 'col'), may hold values from -0.125 to 0.125
- near_index: int32 [2048, 8], P('leaf'), may hold values from 0 to 2047, as said below
- near_count: int32 [2048], P('leaf'), may hold values from 1 to 8, as said below
- leaf_basis: bfloat16 [2048, 64, 256], P('leaf'), may hold values from -0.375 to 0.375
- leaf_coupling: bfloat16 [2048, 64, 256], P('leaf'), may hold values from -0.375 to 0.375
- leaf_far: int32 [2048, 4], P('leaf'), may hold values from 0 to 2047, as said below
- up_leaf: bfloat16 [256, 64, 512], P('leaf'), may hold values from -0.25 to 0.25
- mid_coupling: bfloat16 [256, 64, 256], P('leaf'), may hold values from -0.375 to 0.375
- mid_far: int32 [256, 4], P('leaf'), may hold values from 0 to 255, as said below
- up_mid: bfloat16 [256, 64, 64], P('leaf'), may hold values from -0.75 to 0.75
- top_coupling: bfloat16 [32, 64, 2048], replicated, may hold values from -0.125 to 0.125
Outputs:
- product: float32 [524288, 256], P('leaf', 'col')
Inputs may be any that keep to these rules, and one draw needn't show every extreme that they name: `near_index`: entry 0 of row i is i; the other 7 entries are distinct leaves j with j != i and |i - j| <= 8. Only the first near_count[i] slots of leaf i count; some leaf has all 8. `leaf_far`: row i holds 4 distinct leaves j != i with |i // 8 - j // 8| <= 1. `mid_far`: row a holds 4 distinct middle clusters b != a with |a // 8 - b // 8| <= 1.
All inputs are finite; a program needn't handle non-finite values.
Results may differ from a plain program's by a relative error of at most 0.01.
Values may be sent and summed in bfloat16 or wider, within the bound.
A program may use at most 128 MiB of HBM per device.

v0:
```python
import jax
import jax.numpy as jnp
from jax import lax
from jax.sharding import PartitionSpec as P

CHILD = 8
FAR = 4


def padded(x, sides, width):
    for axis, dim in sides:
        size, length = (lax.axis_size(axis), x.shape[dim])
        up = [(i, (i + 1) % size) for i in range(size - 1)]
        down = [(j, i) for i, j in up]
        last = lax.slice_in_dim(x, length - width, length, axis=dim)
        first = lax.slice_in_dim(x, 0, width, axis=dim)
        before = lax.ppermute(last, axis, up)
        after = lax.ppermute(first, axis, down)
        x = jnp.concatenate([before, x, after], axis=dim)
    return x


def shards(
    sources,
    near_tiles,
    near_index,
    near_count,
    leaf_basis,
    leaf_coupling,
    leaf_far,
    up_leaf,
    mid_coupling,
    mid_far,
    up_mid,
    top_coupling,
):
    f32 = jnp.float32
    bf16 = jnp.bfloat16
    leaf_count = leaf_basis.shape[0]
    rank_size = leaf_basis.shape[1]
    leaf_size = leaf_basis.shape[2]
    col_count = sources.shape[1]
    mid_count = leaf_count // CHILD
    total_top = top_coupling.shape[0]
    device = lax.axis_index("leaf")
    first_leaf = device * leaf_count
    first_mid = device * mid_count
    window = padded(sources, (("leaf", 0),), CHILD * leaf_size)
    near_local = near_index - (first_leaf - CHILD)
    all_tiles = lax.all_gather(near_tiles, "col", axis=1, tiled=True)
    slot_count = all_tiles.shape[1]
    blocks = window.reshape(-1, leaf_size, window.shape[1])
    picked = blocks[near_local]
    live_mask = jnp.arange(slot_count)[None, :] < near_count[:, None]
    picked = jnp.where(live_mask[:, :, None, None], picked, jnp.zeros((), bf16))
    result = jnp.einsum("lsij,lsjc->lic", all_tiles, picked, preferred_element_type=f32)
    near_part = result.reshape(leaf_count * leaf_size, window.shape[1])
    leaf_blocks = sources.reshape(leaf_count, leaf_size, col_count)
    leaf_coef = jnp.einsum(
        "lrk,lkc->lrc", leaf_basis, leaf_blocks, preferred_element_type=f32
    ).astype(bf16)
    mid_coef = jnp.einsum(
        "qrk,qkc->qrc",
        up_leaf,
        leaf_coef.reshape(mid_count, CHILD * rank_size, col_count),
        preferred_element_type=f32,
    ).astype(bf16)
    mid_lift = jnp.einsum("qrs,qsc->qrc", up_mid, mid_coef, preferred_element_type=f32).astype(bf16)
    parent = (first_mid + jnp.arange(mid_count)) // CHILD
    mid_flat = mid_far.reshape(-1)
    top_range = jnp.arange(total_top)
    coef_piece = lax.all_gather(mid_coef, "leaf", axis=0, tiled=True)
    lift_piece = lax.all_gather(mid_lift, "leaf", axis=0, tiled=True)
    global_ids = jnp.arange(coef_piece.shape[0])
    group_map = (top_range[:, None] == (global_ids // CHILD)[None, :]).astype(bf16)
    top_total = jnp.einsum("pk,krc->prc", group_map, lift_piece, preferred_element_type=f32)
    global_ids = jnp.arange(coef_piece.shape[0])
    pick_map = (mid_flat[:, None] == global_ids[None, :]).astype(bf16)
    mid_picked = jnp.einsum("ik,krc->irc", pick_map, coef_piece, preferred_element_type=f32)
    top_coef = top_total.astype(bf16)
    parent_rows = top_coupling[parent]
    keep_mask = top_range[None, :] != parent[:, None]
    stacked = jnp.where(keep_mask[:, :, None, None], top_coef[None], jnp.zeros((), bf16))
    top_field = jnp.einsum(
        "qrk,qkc->qrc",
        parent_rows,
        stacked.reshape(mid_count, total_top * rank_size, col_count),
        preferred_element_type=f32,
    ).astype(bf16)
    mid_chosen = mid_picked.astype(bf16).reshape(mid_count, FAR * rank_size, col_count)
    mid_field = (
        jnp.einsum("qrk,qkc->qrc", mid_coupling, mid_chosen, preferred_element_type=f32)
        + jnp.einsum("qrs,qrc->qsc", up_mid, top_field, preferred_element_type=f32)
    ).astype(bf16)
    leaf_window = padded(leaf_coef, (("leaf", 0),), CHILD)
    far_local = leaf_far - (first_leaf - CHILD)
    leaf_chosen = leaf_window[far_local].reshape(leaf_count, FAR * rank_size, col_count)
    down_part = jnp.einsum("qrs,qrc->qsc", up_leaf, mid_field, preferred_element_type=f32).reshape(
        leaf_count, rank_size, col_count
    )
    leaf_field = (
        jnp.einsum("lrk,lkc->lrc", leaf_coupling, leaf_chosen, preferred_element_type=f32)
        + down_part
    ).astype(bf16)
    far_part = jnp.einsum(
        "lrk,lrc->lkc", leaf_basis, leaf_field, preferred_element_type=f32
    ).reshape(leaf_count * leaf_size, col_count)
    return near_part + far_part


def solution(mesh):
    return jax.shard_map(
        shards,
        mesh=mesh,
        in_specs=(
            P("leaf", "col"),
            P("leaf", "col", None, None),
            P("leaf", None),
            P("leaf"),
            P("leaf", None, None),
            P("leaf", None, None),
            P("leaf", None),
            P("leaf", None, None),
            P("leaf", None, None),
            P("leaf", None),
            P("leaf", None, None),
            P(),
        ),
        out_specs=P("leaf", "col"),
        check_vma=False,
    )
```

profile of v0, /device:TPU:1, one launch (start us, length us, event | category | flops | bytes accessed | tf_op | source)
XLA Modules:
  0.0 305.8 jit_solution(7438297969779662554)
XLA Ops:
  6.5 0.0 copy-start
  6.5 0.0 all-gather.8.cloned.1.call-start
  6.5 1.0 copy-done
  7.6 1.5 convolution_convert_fusion
  9.1 1.1 convolution_convert_fusion.3
  10.2 0.0 copy-start.5
  10.2 1.5 fusion.21
  11.7 0.0 all-gather.8.cloned.1.call-update
  11.7 0.0 all-gather.6.cloned.1.call-start
  11.8 0.0 copy-done.5
  11.8 0.7 all-gather.6.cloned.1.call-update
  12.5 0.0 copy-start.1
  12.5 0.0 copy-start.9
  12.5 0.0 copy-start.12
  12.5 0.0 copy-start.8
  12.5 0.0 all-gather.4.cloned.1.call-start
  12.6 0.7 all-gather.4.cloned.1.call-update
  13.3 0.7 fusion.42
  14.0 5.0 %collective-permute-start.2 = (bf16[8,64,128]{2,1,0:T(8,128)(2,1)}, bf16[8,64,128]{2,1,0:T(8,128)(2,1)}, u32[]{:S(2)}, u32[]{:S(2)}) collective-permute-start(bf16[8,64,128]{2,1,0:T(8,128)(2,1)} %get-tuple-element.7), channel_id=1, source_target_pairs={{0,2},{2,4},{4,6},{6,8},{8,10},{10,12},{12,14},{14,16},{16,18},{18... | collective-permute-start | bytes 393224 | tf_op jit(solution)/shard_map/ppermute | solution.py:17
  19.0 1.3 collective-permute-start.3
  20.3 0.0 copy-done.1
  20.3 0.1 fusion.41
  20.3 4.0 %collective-permute-start = (bf16[2048,128]{1,0:T(8,128)(2,1)S(1)}, bf16[2048,128]{1,0:T(8,128)(2,1)S(1)}, u32[]{:S(2)}, u32[]{:S(2)}) collective-permute-start(bf16[2048,128]{1,0:T(8,128)(2,1)S(1)} %get-tuple-element.5), channel_id=1, source_target_pairs={{0,2},{2,4},{4,6},{6,8},{8,10},{10,12},{12,14},{14,16},{16,18},{18... | collective-permute-start | bytes 1572872 | tf_op jit(solution)/shard_map/ppermute | solution.py:17
  24.4 1.3 collective-permute-start.1
  25.7 0.0 copy-done.9
  25.7 0.1 copy.27
  25.8 0.1 reshape.160
  26.0 0.1 iota_compare_fusion.2
  26.0 0.1 iota_compare_fusion.3
  26.1 0.6 and_select_fusion
  26.7 0.1 broadcast_in_dim.59
  26.8 0.1 broadcast_in_dim.60
  26.9 1.4 eq.28
  28.2 0.1 copy.25
  28.3 0.1 reshape.152
  28.4 4.8 %gather_fusion.2 = bf16[2,64,2048]{2,1,0:T(8,128)(2,1)} fusion(bf16[32,64,2048]{2,1,0:T(8,128)(2,1)} %param.23, s32[1024]{0:T(1024)S(1)} %pad_clamp_fusion), kind=kCustom, calls=%fused_computation.2 | custom fusion | bytes 1048584 | tf_op jit(solution)/shard_map/gather | solution.py:81
  33.2 0.0 collective-permute-done.2
  33.2 0.0 collective-permute-done.3
  33.2 1.0 pad_maximum_fusion.1
  34.2 1.7 gather_fusion.1
  35.9 0.0 collective-permute-done
  35.9 2.6 collective-permute-done.1
  38.5 1.5 pad_maximum_fusion
  40.0 6.6 %gather_fusion = bf16[128,256,128]{2,1,0:T(8,128)(2,1)} fusion(bf16[32,256,128]{2,1,0:T(8,128)(2,1)S(1)} %bitcast.52, s32[1024]{0:T(1024)S(1)} %pad_clamp_fusion.2), kind=kCustom, calls=%fused_computation | custom fusion | bytes 16777728 | tf_op jit(solution)/shard_map/gather | solution.py:53
  46.6 12.0 %copy.26 = bf16[128,256,128]{1,2,0:T(8,128)(2,1)} copy(bf16[128,256,128]{2,1,0:T(8,128)(2,1)} %gather_fusion) | data formatting | bytes 16777216 | tf_op jit(solution)/shard_map/gather | solution.py:53
  58.6 70.6 %all-gather.8.cloned.1.call-done = bf16[256,64,128]{2,1,0:T(8,128)(2,1)} async-done(((bf16[2,64,128]{2,1,0:T(8,128)(2,1)}), bf16[256,64,128]{2,1,0:T(8,128)(2,1)}) %all-gather.8.cloned.1.call-update) | async-done | bytes 4194320 | tf_op jit(solution)/shard_map/all_gather | solution.py:73
  129.2 4.6 %fusion.11 = bf16[32,64,128]{2,0,1:T(8,128)(2,1)S(1)} fusion(bf16[256,64,128]{2,1,0:T(8,128)(2,1)} %all-gather.8.cloned.1.call-done, s32[256]{0:T(256)S(1)} %copy-done.10), kind=kOutput, calls=%fused_computation.14 | convolution fusion | flops 134488064 | bytes 4719616 | tf_op jit(solution)/shard_map/pk,krc->prc/dot_general | solution.py:76
  133.8 0.0 copy-start.4
  133.9 0.0 copy-start.6
  133.9 0.2 copy.31
  134.1 0.0 copy-start.2
  134.1 0.0 copy-start.3
  134.1 112.7 %all-gather.6.cloned.1.call-done = bf16[256,64,128]{2,1,0:T(8,128)(2,1)} async-done(((bf16[2,64,128]{2,1,0:T(8,128)(2,1)}), bf16[256,64,128]{2,1,0:T(8,128)(2,1)}) %all-gather.6.cloned.1.call-update) | async-done | bytes 4194320 | tf_op jit(solution)/shard_map/all_gather | solution.py:72
  246.9 4.5 %fusion.17 = bf16[8,64,128]{2,0,1:T(8,128)(2,1)S(1)} fusion(bf16[256,64,128]{2,1,0:T(8,128)(2,1)} %all-gather.6.cloned.1.call-done, s32[8]{0:T(128)S(1)} %copy-done.11), kind=kOutput, calls=%fused_computation.21 | convolution fusion | flops 33622016 | bytes 4325408 | tf_op jit(solution)/shard_map/ik,krc->irc/dot_general | solution.py:79
  251.4 2.0 fusion.22
  253.3 0.0 copy-done.6
  253.3 0.4 convolution_bitcast_fusion.1
  253.7 0.2 copy.33
  253.9 0.0 copy-done.2
  254.0 0.0 copy-done.3
  254.0 1.9 fusion.16
  255.9 29.6 %all-gather.4.cloned.1.call-done = bf16[16,8,256,256]{3,2,1,0:T(8,128)(2,1)} async-done(((bf16[16,4,256,256]{3,2,1,0:T(8,128)(2,1)}), bf16[16,8,256,256]{3,2,1,0:T(8,128)(2,1)}) %all-gather.4.cloned.1.call-update) | async-done | bytes 16777232 | tf_op jit(solution)/shard_map/all_gather | solution.py:50
  285.5 11.9 %fusion.8 = f32[16,256,128]{1,2,0:T(8,128)S(1)} fusion(f32[16,128,256]{2,1,0:T(8,128)} %fusion.16, bf16[16,8,256,256]{3,2,1,0:T(8,128)(2,1)} %all-gather.4.cloned.1.call-done, bf16[16,8,256,128]{2,3,1,0:T(8,128)(2,1)} %bitcast.54, pred[16,8]{1,0:T(8,128)(4,1)S(1)} %iota_compare_fusion.2), kind=kOutput, calls=%fused_computation.13 | convolution fusion | flops 2152202240 | bytes 29360256 | tf_op jit(solution)/shard_map/lsij,lsjc->lic/dot_general | solution.py:56
  297.4 1.8 copy.34
  (17 shorter events, 0.1 us)
Async XLA Ops:
  6.5 1.0 copy-start
  6.5 122.7 %all-gather.8.cloned.1.call-start = ((), (), s32[]{:S(2)}) async-start(), calls=%async_computation.2 | async-start | bytes 4227072 | tf_op jit(solution)/shard_map/all_gather | solution.py:73
  10.2 1.6 copy-start.5
  11.7 235.1 %all-gather.6.cloned.1.call-start = ((), (), s32[]{:S(2)}) async-start(), calls=%async_computation.1 | async-start | bytes 4227072 | tf_op jit(solution)/shard_map/all_gather | solution.py:72
  12.5 7.8 %copy-start.1 = (bf16[4096,128]{1,0:T(8,128)(2,1)S(1)}, bf16[4096,128]{1,0:T(8,128)(2,1)}, u32[]{:S(2)}) copy-start(bf16[4096,128]{1,0:T(8,128)(2,1)} %param.12) | copy-start | bytes 3145732
  12.5 13.2 %copy-start.9 = (s32[16,4]{0,1:T(4,128)S(1)}, s32[16,4]{0,1:T(4,128)}, u32[]{:S(2)}) copy-start(s32[16,4]{0,1:T(4,128)} %param.18) | copy-start | bytes 772
  12.5 13.4 %copy-start.12 = (s32[16]{0:T(128)S(1)}, s32[16]{0:T(128)}, u32[]{:S(2)}) copy-start(s32[16]{0:T(128)} %param.15) | copy-start | bytes 196
  12.5 13.5 %copy-start.8 = (s32[16,8]{0,1:T(8,128)S(1)}, s32[16,8]{0,1:T(8,128)}, u32[]{:S(2)}) copy-start(s32[16,8]{0,1:T(8,128)} %param.14) | copy-start | bytes 1540
  12.5 273.0 %all-gather.4.cloned.1.call-start = ((), (), s32[]{:S(2)}) async-start(), calls=%async_computation | async-start | bytes 25165824 | tf_op jit(solution)/shard_map/all_gather | solution.py:50
  14.0 19.2 %collective-permute-start.2 = (bf16[8,64,128]{2,1,0:T(8,128)(2,1)}, bf16[8,64,128]{2,1,0:T(8,128)(2,1)}, u32[]{:S(2)}, u32[]{:S(2)}) collective-permute-start(bf16[8,64,128]{2,1,0:T(8,128)(2,1)} %get-tuple-element.7), channel_id=1, source_target_pairs={{0,2},{2,4},{4,6},{6,8},{8,10},{10,12},{12,14},{14,16},{16,18},{18... | collective-permute-start | bytes 393224 | tf_op jit(solution)/shard_map/ppermute | solution.py:17
  19.0 14.2 %collective-permute-start.3 = (bf16[8,64,128]{2,1,0:T(8,128)(2,1)S(1)}, bf16[8,64,128]{2,1,0:T(8,128)(2,1)}, u32[]{:S(2)}, u32[]{:S(2)}) collective-permute-start(bf16[8,64,128]{2,1,0:T(8,128)(2,1)S(1)} %get-tuple-element.8), channel_id=1, source_target_pairs={{2,0},{4,2},{6,4},{8,6},{10,8},{12,10},{14,12},{16,14},{18,16},{20... | collective-permute-start | bytes 393224 | tf_op jit(solution)/shard_map/ppermute | solution.py:18
  20.3 15.5 %collective-permute-start = (bf16[2048,128]{1,0:T(8,128)(2,1)S(1)}, bf16[2048,128]{1,0:T(8,128)(2,1)S(1)}, u32[]{:S(2)}, u32[]{:S(2)}) collective-permute-start(bf16[2048,128]{1,0:T(8,128)(2,1)S(1)} %get-tuple-element.5), channel_id=1, source_target_pairs={{0,2},{2,4},{4,6},{6,8},{8,10},{10,12},{12,14},{14,16},{16,18},{18... | collective-permute-start | bytes 1572872 | tf_op jit(solution)/shard_map/ppermute | solution.py:17
  24.4 14.1 %collective-permute-start.1 = (bf16[2048,128]{1,0:T(8,128)(2,1)S(1)}, bf16[2048,128]{1,0:T(8,128)(2,1)}, u32[]{:S(2)}, u32[]{:S(2)}) collective-permute-start(bf16[2048,128]{1,0:T(8,128)(2,1)S(1)} %get-tuple-element.6), channel_id=1, source_target_pairs={{2,0},{4,2},{6,4},{8,6},{10,8},{12,10},{14,12},{16,14},{18,16},{20... | collective-permute-start | bytes 1572872 | tf_op jit(solution)/shard_map/ppermute | solution.py:18
  46.6 82.6 %copy-start.10 = (s32[256]{0:T(256)S(1)}, s32[256]{0:T(256)}, u32[]{:S(2)}) copy-start(s32[256]{0:T(256)} %and_select_fusion) | copy-start | bytes 3076
  58.6 188.3 %copy-start.11 = (s32[8]{0:T(128)S(1)}, s32[8]{0:T(128)}, u32[]{:S(2)}) copy-start(s32[8]{0:T(128)} %eq.28) | copy-start | bytes 100
  58.6 192.8 %copy-start.7 = (bf16[2,64,64]{2,1,0:T(8,128)(2,1)S(1)}, bf16[2,64,64]{2,1,0:T(8,128)(2,1)}, u32[]{:S(2)}) copy-start(bf16[2,64,64]{2,1,0:T(8,128)(2,1)} %param.22) | copy-start | bytes 49156
  133.8 119.5 %copy-start.4 = (bf16[2,64,512]{2,1,0:T(8,128)(2,1)S(1)}, bf16[2,64,512]{2,1,0:T(8,128)(2,1)}, u32[]{:S(2)}) copy-start(bf16[2,64,512]{2,1,0:T(8,128)(2,1)} %param.19) | copy-start | bytes 393220
  133.9 119.5 %copy-start.6 = (bf16[2,64,256]{2,1,0:T(8,128)(2,1)S(1)}, bf16[2,64,256]{2,1,0:T(8,128)(2,1)}, u32[]{:S(2)}) copy-start(bf16[2,64,256]{2,1,0:T(8,128)(2,1)} %param.20) | copy-start | bytes 196612
  134.1 119.9 %copy-start.2 = (bf16[64,64,128]{2,1,0:T(8,128)(2,1)S(1)}, bf16[64,64,128]{2,1,0:T(8,128)(2,1)}, u32[]{:S(2)}) copy-start(bf16[64,64,128]{2,1,0:T(8,128)(2,1)} %gather_fusion.1) | copy-start | bytes 3145732
  134.1 119.9 %copy-start.3 = (bf16[16,64,256]{2,1,0:T(8,128)(2,1)S(1)}, bf16[16,64,256]{2,1,0:T(8,128)(2,1)}, u32[]{:S(2)}) copy-start(bf16[16,64,256]{2,1,0:T(8,128)(2,1)} %param.17) | copy-start | bytes 1572868
Sparse Core Ops, SparseCore 0:
  11.9 117.2 all-gather.7
  132.8 113.9 all-gather.5
  248.7 36.8 all-gather.3
where the time goes:
time: 307 us; the launch traced here: 306 us
  waiting for transfers between devices  217 us (71%)
  local copies, waits for them, and re-layouts  30.9 us (10%)
  matrix products  29.4 us (10%)
  between operations  13.4 us (4%)
  starting transfers between devices  11.7 us (4%)
  other arithmetic  3.34 us (1%)
    all_gather x1, waiting for transfers between devices, shards(): coef_piece = lax.all_gather(mid_coef, 'leaf', axis=0, tiled=True)  113 us
    all_gather x1, waiting for transfers between devices, shards(): lift_piece = lax.all_gather(mid_lift, 'leaf', axis=0, tiled=True)  70.6 us
    all_gather x1, waiting for transfers between devices, shards(): all_tiles = lax.all_gather(near_tiles, 'col', axis=1, tiled=True)  29.6 us
    gather x2, local copies, waits for them, and re-layouts, shards(): picked = blocks[near_local]  18.6 us
    dot_general x1, matrix products, shards(): jnp.einsum('lsij,lsjc->lic', all_tiles, picked, preferred_element_type=f32)  11.9 us
    ppermute x2, starting transfers between devices, padded(): before = lax.ppermute(last, axis, up)  9.04 us
  transfers between devices with their start and end apart: 7, of which 4 were waited for; matrix products, arithmetic and copies ran while one was open for 15% of the time, Pallas kernels for 0%

commit v1 on v0

v1 whole, which is shorter than its diff:
```python
import functools

import jax
import jax.numpy as jnp
from jax import lax
from jax.experimental import pallas as pl
from jax.experimental.pallas import tpu as pltpu
from jax.sharding import PartitionSpec as P

MESH = pl.DeviceIdType.MESH
F32 = jnp.float32
BF16 = jnp.bfloat16

LEAF = 256
RANK = 64
HALF = 128
OWN = 16
HALO = 8
MIDS = 2
GROUP = 4
TOPS = 32
SLOTS = 4
ZERO = OWN + 2 * HALO
CHUNK = 2
CHUNKS = HALO // CHUNK


def dot(a, b):
    return jnp.dot(a, b, preferred_element_type=F32)


def dot_t(a, b):
    return lax.dot_general(a, b, (((0,), (0,)), ((), ())), preferred_element_type=F32)


def kernel(
    src, tiles, near_index, near_count, basis, coupling, leaf_far, up_leaf, mid_coupling, mid_far, up_mid, top_coupling,
    out,
    w0, w1, tile, bas, cpl, upl, mcp, upm, top, coef, mid, part, top_a, coef_top, top_b, field, top_c, mfield,
    lfield, near, give, take,
    load_sem, tile_sem, out_sem, sib_send, sib_recv, halo_send, halo_recv, fwd_send, fwd_recv,
    coef_send, coef_recv, mid_send, mid_recv, a_send, a_recv, b_send, b_recv, c_send, c_recv, give_send, give_recv,
):
    d, c = lax.axis_index("leaf"), lax.axis_index("col")
    devices = TOPS * GROUP
    g, r = d // GROUP, d % GROUP
    z, x, y = g % 2, (g // 2) % 4, g // 8
    sibling = (d, 1 - c)
    after, before = ((d + 1) % devices, c), ((d + devices - 1) % devices, c)

    def member(group, k):
        return (group * GROUP + k, c)

    mates = [member(g, (r + o) % GROUP) for o in (1, 2, 3)]
    sides = [member((g + o) % TOPS, k) for o in (1, TOPS - 1) for k in range(GROUP)]
    far_x, far_r = (x + r) % 4, (GROUP - r) % GROUP
    peers = [(j, zt, member((((y + j) % 4) * 4 + far_x) * 2 + zt, far_r)) for j in range(4) for zt in range(2)]

    def copy(a, b, send, recv, device):
        return pltpu.make_async_remote_copy(
            src_ref=a, dst_ref=b, send_sem=send, recv_sem=recv, device_id=device, device_id_type=MESH
        )

    def not_self(j, zt, body):
        if j == 0:
            pl.when(jnp.logical_or(r != 0, z != zt))(body)
        else:
            body()

    barrier = pltpu.get_barrier_semaphore()

    def greet(device):
        pl.semaphore_signal(barrier, inc=1, device_id=device, device_id_type=MESH)

    for device in [sibling] + mates + sides:
        greet(device)
    for j, zt, device in peers:
        not_self(j, zt, functools.partial(greet, device))

    loads = [
        pltpu.make_async_copy(src, w0.at[pl.ds(HALO, OWN)], load_sem.at[0]),
        pltpu.make_async_copy(basis, bas, load_sem.at[1]),
        pltpu.make_async_copy(up_leaf, upl, load_sem.at[2]),
        pltpu.make_async_copy(up_mid, upm, load_sem.at[3]),
        pltpu.make_async_copy(coupling, cpl, load_sem.at[4]),
        pltpu.make_async_copy(mid_coupling, mcp, load_sem.at[5]),
    ]
    for j in range(4):
        pair = ((y + j) % 4) * 4 + far_x
        loads.append(
            pltpu.make_async_copy(
                top_coupling.at[g, :, pl.ds(pl.multiple_of(pair * 2 * RANK, 2 * RANK), 2 * RANK)],
                top.at[j],
                load_sem.at[6 + j],
            )
        )
    for load in loads:
        load.start()
    tile_loads = [
        pltpu.make_async_copy(tiles.at[pl.ds(4 * k, 4)], tile.at[pl.ds(4 * k, 4)], tile_sem.at[k]) for k in range(4)
    ]
    for load in tile_loads:
        load.start()

    zero = jnp.zeros((LEAF, HALF), BF16)
    w0[ZERO] = zero
    w1[ZERO] = zero

    @pl.when(r == 0)
    def _():
        top_b[0, z] = jnp.zeros((RANK, HALF), BF16)
        pl.semaphore_wait(barrier, 19)

    @pl.when(r != 0)
    def _():
        pl.semaphore_wait(barrier, 20)

    to_sibling = copy(src, w1.at[pl.ds(HALO, OWN)], sib_send, sib_recv, sibling)
    to_after, to_before, fwd_low, fwd_high = [], [], [], []
    for i in range(CHUNKS):
        low = pl.ds(HALO - CHUNK * (i + 1), CHUNK)
        high = pl.ds(HALO + OWN + CHUNK * i, CHUNK)
        to_after.append(
            copy(src.at[pl.ds(OWN - CHUNK * (i + 1), CHUNK)], w0.at[low], halo_send.at[0, i], halo_recv.at[0, i], after)
        )
        to_before.append(
            copy(src.at[pl.ds(CHUNK * i, CHUNK)], w0.at[high], halo_send.at[1, i], halo_recv.at[1, i], before)
        )
        fwd_low.append(copy(w0.at[low], w1.at[low], fwd_send.at[0, i], fwd_recv.at[0, i], sibling))
        fwd_high.append(copy(w0.at[high], w1.at[high], fwd_send.at[1, i], fwd_recv.at[1, i], sibling))
    for i in range(CHUNKS):
        to_after[i].start()
        to_before[i].start()
    to_sibling.start()

    loads[0].wait()
    loads[1].wait()

    def leaf_step(i, _):
        coef[HALO + i] = dot(bas[i], w0[HALO + i]).astype(BF16)
        return 0

    lax.fori_loop(0, OWN, leaf_step, 0)
    coef_out = [
        copy(coef.at[pl.ds(OWN, HALO)], coef.at[pl.ds(0, HALO)], coef_send.at[0], coef_recv.at[0], after),
        copy(coef.at[pl.ds(HALO, HALO)], coef.at[pl.ds(HALO + OWN, HALO)], coef_send.at[1], coef_recv.at[1], before),
    ]

    loads[2].wait()
    loads[3].wait()
    own_mid = pl.ds(MIDS * (GROUP + r), MIDS)
    total = None
    for q in range(MIDS):
        rows = coef[pl.ds(HALO + 8 * q, 8)].reshape(8 * RANK, HALF)
        value = dot(upl[q], rows).astype(BF16)
        mid[MIDS * (GROUP + r) + q] = value
        lift = dot(upm[q], value).astype(BF16).astype(F32)
        total = lift if total is None else total + lift
    part[...] = total
    to_mates = [copy(part, top_a.at[o], a_send.at[o], a_recv.at[o], mates[o]) for o in range(3)]
    for one in to_mates:
        one.start()
    mid_out = []
    for o in range(3):
        mid_out.append(copy(mid.at[own_mid], mid.at[own_mid], mid_send.at[o], mid_recv.at[GROUP + r], mates[o]))
    for o, base in ((0, 0), (1, 2 * GROUP)):
        there = pl.ds(MIDS * (base + r), MIDS)
        for k in range(GROUP):
            n = 3 + GROUP * o + k
            mid_out.append(
                copy(mid.at[own_mid], mid.at[there], mid_send.at[n], mid_recv.at[base + r], sides[GROUP * o + k])
            )
    for one in coef_out:
        one.start()
    for one in mid_out:
        one.start()

    for one in to_mates:
        one.wait_recv()
    coef_top[...] = (part[...] + top_a[0] + top_a[1] + top_a[2]).astype(BF16)
    to_peers = []
    for j, zt, device in peers:
        one = copy(
            coef_top, top_b.at[(4 - j) % 4, z], b_send.at[j, zt], b_recv.at[(4 - j) % 4, z], device
        )
        to_peers.append((j, zt, one))
        not_self(j, zt, one.start)

    for i in range(2):
        to_after[i].wait_recv()
        to_before[i].wait_recv()
        fwd_low[i].start()
        fwd_high[i].start()
    loads[4].wait()
    for one in coef_out:
        one.wait_recv()

    def far_step(i, _):
        picked = [coef[jnp.clip(leaf_far[i, f] - (d * OWN - HALO), 0, ZERO - 1)] for f in range(4)]
        lfield[i] = dot(cpl[i], jnp.concatenate(picked, axis=0))
        return 0

    lax.fori_loop(0, OWN, far_step, 0)

    for j in range(4):
        loads[6 + j].wait()
    for j, zt, _ in peers:
        got = copy(coef_top, top_b.at[j, zt], b_send.at[j, zt], b_recv.at[j, zt], sibling)
        not_self(j, zt, got.wait_recv)
    total = dot(top[0], top_b[0].reshape(2 * RANK, HALF))
    for j in range(1, 4):
        total = total + dot(top[j], top_b[j].reshape(2 * RANK, HALF))
    field[...] = total
    fields_out = [copy(field, top_c.at[o], c_send.at[o], c_recv.at[o], mates[o]) for o in range(3)]
    for one in fields_out:
        one.start()

    for k in range(3 * GROUP):
        here = mid.at[pl.ds(MIDS * k, MIDS)]
        got = copy(here, here, mid_send.at[0], mid_recv.at[k], sibling)
        if k // GROUP == 1:
            pl.when(k != GROUP + r)(got.wait_recv)
        else:
            got.wait_recv()
    loads[5].wait()
    first = (g - 1) * 8
    for q in range(MIDS):
        picked = [mid[jnp.clip(mid_far[q, f] - first, 0, 3 * GROUP * MIDS - 1)] for f in range(4)]
        mfield[q] = dot(mcp[q], jnp.concatenate(picked, axis=0))
    for one in fields_out:
        one.wait_recv()
    top_field = (field[...] + top_c[0] + top_c[1] + top_c[2]).astype(BF16)
    for q in range(MIDS):
        value = (mfield[q] + dot_t(upm[q], top_field)).astype(BF16)
        down = dot_t(upl[q], value).reshape(8, RANK, HALF)
        lfield[pl.ds(8 * q, 8)] = lfield[pl.ds(8 * q, 8)] + down

    for i in range(2, CHUNKS):
        to_after[i].wait_recv()
        to_before[i].wait_recv()
        fwd_low[i].start()
        fwd_high[i].start()

    def product_step(i, _):
        near[i] = dot_t(bas[i], lfield[i].astype(BF16))
        return 0

    lax.fori_loop(0, OWN, product_step, 0)

    to_sibling.wait_recv()
    for i in range(CHUNKS):
        fwd_low[i].wait_recv()
        fwd_high[i].wait_recv()
    for load in tile_loads:
        load.wait()

    def give_copy(i):
        return copy(give.at[i], take.at[i], give_send.at[i], give_recv.at[i], sibling)

    def near_step(i, _):
        total = None
        for s in range(SLOTS):
            slot = c * SLOTS + s
            j = jnp.clip(near_index[i, slot] - (d * OWN - HALO), 0, ZERO - 1)
            j = jnp.where(slot < near_count[i], j, ZERO)
            rows = jnp.concatenate([w0[j], w1[j]], axis=1)
            term = dot(tile[i, s], rows)
            total = term if total is None else total + term
        near[i] = near[i] + total[:, :HALF]
        give[i] = total[:, HALF:].astype(BF16)
        give_copy(i).start()
        return 0

    lax.fori_loop(0, OWN, near_step, 0)

    def finish(i, _):
        give_copy(i).wait_recv()
        near[i] = near[i] + take[i].astype(F32)
        pltpu.make_async_copy(near.at[i], out.at[i], out_sem.at[i]).start()
        return 0

    lax.fori_loop(0, OWN, finish, 0)

    def drain(i, _):
        pltpu.make_async_copy(near.at[i], out.at[i], out_sem.at[i]).wait()
        give_copy(i).wait_send()
        return 0

    lax.fori_loop(0, OWN, drain, 0)
    to_sibling.wait_send()
    for one in to_after + to_before + fwd_low + fwd_high + coef_out + mid_out + to_mates + fields_out:
        one.wait_send()
    for j, zt, one in to_peers:
        not_self(j, zt, one.wait_send)


def shards(
    sources, near_tiles, near_index, near_count, leaf_basis, leaf_coupling, leaf_far, up_leaf, mid_coupling, mid_far,
    up_mid, top_coupling,
):
    any_spec = pl.BlockSpec(memory_space=pl.ANY)
    smem_spec = pl.BlockSpec(memory_space=pltpu.SMEM)
    dma, vmem = pltpu.SemaphoreType.DMA, pltpu.VMEM
    window = OWN + 2 * HALO
    result = pl.pallas_call(
        kernel,
        out_shape=jax.ShapeDtypeStruct((OWN, LEAF, HALF), F32),
        in_specs=[
            any_spec, any_spec, smem_spec, smem_spec, any_spec, any_spec, smem_spec, any_spec, any_spec, smem_spec,
            any_spec, any_spec,
        ],
        out_specs=any_spec,
        scratch_shapes=[
            vmem((window + 1, LEAF, HALF), BF16),
            vmem((window + 1, LEAF, HALF), BF16),
            vmem((OWN, SLOTS, LEAF, LEAF), BF16),
            vmem((OWN, RANK, LEAF), BF16),
            vmem((OWN, RANK, 4 * RANK), BF16),
            vmem((MIDS, RANK, 8 * RANK), BF16),
            vmem((MIDS, RANK, 4 * RANK), BF16),
            vmem((MIDS, RANK, RANK), BF16),
            vmem((4, RANK, 2 * RANK), BF16),
            vmem((window, RANK, HALF), BF16),
            vmem((3 * GROUP * MIDS, RANK, HALF), BF16),
            vmem((RANK, HALF), F32),
            vmem((3, RANK, HALF), F32),
            vmem((RANK, HALF), BF16),
            vmem((4, 2, RANK, HALF), BF16),
            vmem((RANK, HALF), F32),
            vmem((3, RANK, HALF), F32),
            vmem((MIDS, RANK, HALF), F32),
            vmem((OWN, RANK, HALF), F32),
            vmem((OWN, LEAF, HALF), F32),
            vmem((OWN, LEAF, HALF), BF16),
            vmem((OWN, LEAF, HALF), BF16),
            dma((10,)), dma((4,)), dma((OWN,)),
            dma(()), dma(()),
            dma((2, CHUNKS)), dma((2, CHUNKS)),
            dma((2, CHUNKS)), dma((2, CHUNKS)),
            dma((2,)), dma((2,)),
            dma((11,)), dma((3 * GROUP,)),
            dma((3,)), dma((3,)),
            dma((4, 2)), dma((4, 2)),
            dma((3,)), dma((3,)),
            dma((OWN,)), dma((OWN,)),
        ],
        compiler_params=pltpu.CompilerParams(
            collective_id=0, has_side_effects=True, vmem_limit_bytes=48 * 2**20
        ),
        name="h2_product",
    )(
        sources.reshape(OWN, LEAF, HALF), near_tiles, near_index, near_count, leaf_basis, leaf_coupling, leaf_far,
        up_leaf, mid_coupling, mid_far, up_mid, top_coupling,
    )
    return result.reshape(OWN * LEAF, HALF)


def solution(mesh):
    return jax.shard_map(
        shards,
        mesh=mesh,
        in_specs=(
            P("leaf", "col"),
            P("leaf", "col", None, None),
            P("leaf", None),
            P("leaf"),
            P("leaf", None, None),
            P("leaf", None, None),
            P("leaf", None),
            P("leaf", None, None),
            P("leaf", None, None),
            P("leaf", None),
            P("leaf", None, None),
            P(),
        ),
        out_specs=P("leaf", "col"),
        check_vma=False,
    )
```

time: 307 us -> 71.6 us (0.23)
  the two profiles are of different devices: /device:TPU:1 before, /device:TPU:4 now
where the time goes in v1:
time: 71.6 us; the launch traced here: 71.2 us
  Pallas kernels  61.2 us (85%)
  local copies, waits for them, and re-layouts  9.98 us (14%)
    pallas_call x1, Pallas kernels, shards(): pl.pallas_call(kernel, out_shape=jax.ShapeDtypeStruct((OWN, LEAF, HALF),...  61.2 us
    unnamed x19, local copies, waits for them, and re-layouts  9.98 us

profile of v1, /device:TPU:4, one launch (start us, length us, event | category | flops | bytes accessed | tf_op | source)
XLA Modules:
  0.0 71.2 jit_solution(9989016014217862813)
XLA Ops:
  0.0 0.8 %copy.13.near_index = s32[16,8]{1,0:T(8,128)S(1)} copy(s32[16,8]{0,1:T(8,128)} %param.14) | data formatting | bytes 1024 | tf_op args[2]
  0.8 0.8 %copy.14.leaf_far = s32[16,4]{1,0:T(8,128)S(1)} copy(s32[16,4]{0,1:T(4,128)} %param.18) | data formatting | bytes 512 | tf_op args[6]
  1.5 0.0 copy-start
  1.5 1.2 %copy-done = bf16[4096,128]{1,0:T(8,128)(2,1)S(1)} copy-done((bf16[4096,128]{1,0:T(8,128)(2,1)S(1)}, bf16[4096,128]{1,0:T(8,128)(2,1)}, u32[]{:S(2)}) %copy-start) | copy-done | bytes 1048600
  2.7 0.0 copy-start.1
  2.7 1.0 %copy-done.1 = bf16[16,64,256]{2,1,0:T(8,128)(2,1)S(1)} copy-done((bf16[16,64,256]{2,1,0:T(8,128)(2,1)S(1)}, bf16[16,64,256]{2,1,0:T(8,128)(2,1)}, u32[]{:S(2)}) %copy-start.1) | copy-done | bytes 524312
  3.8 0.0 copy-start.2
  3.8 1.0 %copy-done.2 = bf16[16,64,256]{2,1,0:T(8,128)(2,1)S(1)} copy-done((bf16[16,64,256]{2,1,0:T(8,128)(2,1)S(1)}, bf16[16,64,256]{2,1,0:T(8,128)(2,1)}, u32[]{:S(2)}) %copy-start.2) | copy-done | bytes 524312
  4.8 0.0 copy-start.3
  4.8 0.9 %copy-done.3 = bf16[2,64,512]{2,1,0:T(8,128)(2,1)S(1)} copy-done((bf16[2,64,512]{2,1,0:T(8,128)(2,1)S(1)}, bf16[2,64,512]{2,1,0:T(8,128)(2,1)}, u32[]{:S(2)}) %copy-start.3) | copy-done | bytes 131096
  5.7 0.0 copy-start.4
  5.7 0.8 %copy-done.4 = bf16[2,64,256]{2,1,0:T(8,128)(2,1)S(1)} copy-done((bf16[2,64,256]{2,1,0:T(8,128)(2,1)S(1)}, bf16[2,64,256]{2,1,0:T(8,128)(2,1)}, u32[]{:S(2)}) %copy-start.4) | copy-done | bytes 65560
  6.6 0.0 copy-start.5
  6.6 0.8 %copy-done.5 = bf16[2,64,64]{2,1,0:T(8,128)(2,1)S(1)} copy-done((bf16[2,64,64]{2,1,0:T(8,128)(2,1)S(1)}, bf16[2,64,64]{2,1,0:T(8,128)(2,1)}, u32[]{:S(2)}) %copy-start.5) | copy-done | bytes 16408
  7.3 0.0 copy-start.6
  7.3 0.7 copy-done.6
  8.0 0.0 copy-start.7
  8.0 0.7 copy-done.7
  8.7 61.2 %h2_product.1 = f32[16,256,128]{2,1,0:T(8,128)S(1)} custom-call(bf16[16,256,128]{2,1,0:T(8,128)(2,1)S(1)} %bitcast.3, bf16[16,4,256,256]{3,2,1,0:T(8,128)(2,1)} %tiles.1, s32[16,8]{1,0:T(8,128)S(1)} %copy.13.near_index, s32[16]{0:T(128)S(1)} %copy-done.7, bf16[16,64,256]{2,1,0:T(8,128)(2,1)S(1)} %copy-done.1, bf16[16,64,256]{2,1,0:T(8,128)(2,1)S(1)} %copy-done.2, ...), custom_call_target="tpu_custom_call" | custom-call | tf_op jit(solution)/shard_map/h2_product/pallas_call | solution.py:305
  69.9 1.3 %copy.16 = f32[4096,128]{1,0:T(8,128)} copy(f32[4096,128]{1,0:T(8,128)S(1)} %bitcast.2) | data formatting | bytes 4194304
Async XLA Ops:
  1.5 1.2 %copy-start = (bf16[4096,128]{1,0:T(8,128)(2,1)S(1)}, bf16[4096,128]{1,0:T(8,128)(2,1)}, u32[]{:S(2)}) copy-start(bf16[4096,128]{1,0:T(8,128)(2,1)} %param.12) | copy-start | bytes 3145732
  2.7 1.0 %copy-start.1 = (bf16[16,64,256]{2,1,0:T(8,128)(2,1)S(1)}, bf16[16,64,256]{2,1,0:T(8,128)(2,1)}, u32[]{:S(2)}) copy-start(bf16[16,64,256]{2,1,0:T(8,128)(2,1)} %basis.1) | copy-start | bytes 1572868
  3.8 1.0 %copy-start.2 = (bf16[16,64,256]{2,1,0:T(8,128)(2,1)S(1)}, bf16[16,64,256]{2,1,0:T(8,128)(2,1)}, u32[]{:S(2)}) copy-start(bf16[16,64,256]{2,1,0:T(8,128)(2,1)} %coupling.1) | copy-start | bytes 1572868
  4.8 0.9 %copy-start.3 = (bf16[2,64,512]{2,1,0:T(8,128)(2,1)S(1)}, bf16[2,64,512]{2,1,0:T(8,128)(2,1)}, u32[]{:S(2)}) copy-start(bf16[2,64,512]{2,1,0:T(8,128)(2,1)} %up_leaf.1) | copy-start | bytes 393220
  5.7 0.8 %copy-start.4 = (bf16[2,64,256]{2,1,0:T(8,128)(2,1)S(1)}, bf16[2,64,256]{2,1,0:T(8,128)(2,1)}, u32[]{:S(2)}) copy-start(bf16[2,64,256]{2,1,0:T(8,128)(2,1)} %mid_coupling.1) | copy-start | bytes 196612
  6.6 0.8 %copy-start.5 = (bf16[2,64,64]{2,1,0:T(8,128)(2,1)S(1)}, bf16[2,64,64]{2,1,0:T(8,128)(2,1)}, u32[]{:S(2)}) copy-start(bf16[2,64,64]{2,1,0:T(8,128)(2,1)} %up_mid.1) | copy-start | bytes 49156
  7.3 0.7 copy-start.6
  8.0 0.7 copy-start.7

commit v2 on v1

v2 whole, which is shorter than its diff:
```python
import functools

import jax
import jax.numpy as jnp
from jax import lax
from jax.experimental import pallas as pl
from jax.experimental.pallas import tpu as pltpu
from jax.sharding import PartitionSpec as P

MESH = pl.DeviceIdType.MESH
F32 = jnp.float32
BF16 = jnp.bfloat16

LEAF = 256
RANK = 64
HALF = 128
OWN = 16
HALO = 8
MIDS = 2
GROUP = 4
RING = 8
COLUMNS = 16
SLOTS = 4
WINDOW = OWN + 2 * HALO
CHUNK = 2
CHUNKS = HALO // CHUNK
MID_WINDOW = 4 * GROUP * MIDS


def dot(a, b):
    return jnp.dot(a, b, preferred_element_type=F32)


def dot_t(a, b):
    return lax.dot_general(a, b, (((0,), (0,)), ((), ())), preferred_element_type=F32)


def by_fours(body):
    def step(k, _):
        for i in range(4):
            body(4 * k + i)
        return 0

    lax.fori_loop(0, OWN // 4, step, 0)


def kernel(
    src, tiles, near_index_in, near_count_in, basis, coupling, leaf_far_in, up_leaf, mid_coupling, mid_far_in, up_mid,
    top_coupling,
    near, take,
    near_index, near_count, leaf_far, mid_far,
    w0, w1, tile, bas, cpl, upl, mcp, upm, top, coef, mid, part, top_a, coef_top, top_b, field, top_c, lfield, give,
    load_sem, tile_sem, sib_send, sib_recv, halo_send, halo_recv, fwd_send, fwd_recv, coef_send, coef_recv,
    ring_send, ring_recv, a_send, a_recv, b_send, b_recv, c_send, c_recv, give_send, give_recv,
):
    d, c = lax.axis_index("leaf"), lax.axis_index("col")
    devices = COLUMNS * RING
    g, r = d // GROUP, d % GROUP
    column, z = d // RING, d % RING
    half, x, y = g % 2, column % 4, column // 4
    sibling = (d, 1 - c)
    after, before = ((d + 1) % devices, c), ((d + devices - 1) % devices, c)
    above, below = (column * RING + (z + 1) % RING, c), (column * RING + (z + RING - 1) % RING, c)
    mates = [(g * GROUP + (r + o) % GROUP, c) for o in (1, 2, 3)]
    inner = (r * (3 - r)) // 2
    other = column * RING + (1 - half) * GROUP
    sums = [(g * GROUP + 1, c), (g * GROUP + 2, c), (other, c), (other + 3, c)]
    sum_of = inner * half + (1 - inner) * (1 - half)
    odd = r // 2
    peers = [
        (((((y + 2 * jj + odd) % 4) * 4 + (x + xo) % 4) * RING + z), jj, xo) for jj in range(2) for xo in range(4)
    ]
    across = (((column + 1 - 2 * half + COLUMNS) % COLUMNS) * RING + z, c)
    across_from = (((column - 1 + 2 * half + COLUMNS) % COLUMNS) * RING + z, c)

    def copy(a, b, send, recv, device):
        return pltpu.make_async_remote_copy(
            src_ref=a, dst_ref=b, send_sem=send, recv_sem=recv, device_id=device, device_id_type=MESH
        )

    def if_not(flag, here, body):
        if here:
            pl.when(jnp.logical_not(flag))(body)
        else:
            body()

    barrier = pltpu.get_barrier_semaphore()

    def greet(device):
        pl.semaphore_signal(barrier, inc=1, device_id=device, device_id_type=MESH)

    column_mates = [(column * RING + (z + o) % RING, c) for o in range(1, RING)]
    for device in [sibling, after, before, across, across_from] + column_mates:
        greet(device)
    for device, jj, xo in peers:
        if_not(odd == 0, jj == 0 and xo == 0, functools.partial(greet, (device, c)))

    loads = [
        pltpu.make_async_copy(src, w0.at[pl.ds(HALO, OWN)], load_sem.at[0]),
        pltpu.make_async_copy(basis, bas, load_sem.at[1]),
        pltpu.make_async_copy(up_leaf, upl, load_sem.at[2]),
        pltpu.make_async_copy(up_mid, upm, load_sem.at[3]),
        pltpu.make_async_copy(leaf_far_in, leaf_far, load_sem.at[4]),
        pltpu.make_async_copy(mid_far_in, mid_far, load_sem.at[5]),
        pltpu.make_async_copy(near_index_in, near_index, load_sem.at[6]),
        pltpu.make_async_copy(near_count_in, near_count, load_sem.at[7]),
        pltpu.make_async_copy(coupling, cpl, load_sem.at[8]),
        pltpu.make_async_copy(mid_coupling, mcp, load_sem.at[9]),
    ]
    for device, jj, xo in peers:
        pair = ((y + 2 * jj + odd) % 4) * 4 + (x + xo) % 4
        loads.append(
            pltpu.make_async_copy(
                top_coupling.at[g, :, pl.ds(pl.multiple_of(pair * 2 * RANK, 2 * RANK), 2 * RANK)],
                top.at[4 * jj + xo],
                load_sem.at[10 + 4 * jj + xo],
            )
        )
    for load in loads:
        load.start()
    tile_loads = [
        pltpu.make_async_copy(tiles.at[pl.ds(4 * k, 4)], tile.at[pl.ds(4 * k, 4)], tile_sem.at[k]) for k in range(4)
    ]
    for load in tile_loads:
        load.start()

    zero = jnp.zeros((LEAF, HALF), BF16)
    w0[WINDOW] = zero
    w1[WINDOW] = zero
    for n in range(8):
        top_b[n, 1 - sum_of] = jnp.zeros((RANK, HALF), BF16)

    @pl.when(odd == 0)
    def _():
        top_b[0, sum_of] = jnp.zeros((RANK, HALF), BF16)
        pl.semaphore_wait(barrier, 19)

    @pl.when(odd != 0)
    def _():
        pl.semaphore_wait(barrier, 20)

    to_sibling = copy(src, w1.at[pl.ds(HALO, OWN)], sib_send, sib_recv, sibling)
    to_after, to_before, fwd_low, fwd_high = [], [], [], []
    for i in range(CHUNKS):
        low = pl.ds(HALO - CHUNK * (i + 1), CHUNK)
        high = pl.ds(HALO + OWN + CHUNK * i, CHUNK)
        to_after.append(
            copy(src.at[pl.ds(OWN - CHUNK * (i + 1), CHUNK)], w0.at[low], halo_send.at[0, i], halo_recv.at[0, i], after)
        )
        to_before.append(
            copy(src.at[pl.ds(CHUNK * i, CHUNK)], w0.at[high], halo_send.at[1, i], halo_recv.at[1, i], before)
        )
        fwd_low.append(copy(w0.at[low], w1.at[low], fwd_send.at[0, i], fwd_recv.at[0, i], sibling))
        fwd_high.append(copy(w0.at[high], w1.at[high], fwd_send.at[1, i], fwd_recv.at[1, i], sibling))

    def forward(i):
        to_after[i].wait_recv()
        to_before[i].wait_recv()
        fwd_low[i].start()
        fwd_high[i].start()

    for i in range(CHUNKS):
        to_after[i].start()
        to_before[i].start()
    to_sibling.start()

    loads[0].wait()
    loads[1].wait()

    def leaf_step(i):
        coef[HALO + i] = dot(bas[i], w0[HALO + i]).astype(BF16)

    by_fours(leaf_step)
    coef_out = [
        copy(coef.at[pl.ds(OWN, HALO)], coef.at[pl.ds(0, HALO)], coef_send.at[0], coef_recv.at[0], after),
        copy(coef.at[pl.ds(HALO, HALO)], coef.at[pl.ds(HALO + OWN, HALO)], coef_send.at[1], coef_recv.at[1], before),
    ]

    loads[2].wait()
    loads[3].wait()
    base = GROUP * MIDS
    values = [
        dot(upl[q], coef[pl.ds(HALO + 8 * q, 8)].reshape(8 * RANK, HALF)).astype(BF16) for q in range(MIDS)
    ]
    lifts = [dot(upm[q], values[q]).astype(BF16).astype(F32) for q in range(MIDS)]
    part[...] = (lifts[0] + lifts[1]).astype(BF16)
    for q in range(MIDS):
        mid[base + MIDS * z + q] = values[q]
    sums_out = [copy(part, top_a.at[r], a_send.at[n], a_recv.at[r], sums[n]) for n in range(4)]
    for n in range(4):
        if_not(r == n + 1, n < 2, sums_out[n].start)

    def of(origin):
        return mid.at[pl.ds(base + MIDS * ((origin + RING) % RING), MIDS)]

    ring_up = [copy(of(z - s), of(z - s), ring_send.at[0, s], ring_recv.at[0, s], above) for s in range(4)]
    ring_down = [copy(of(z + s), of(z + s), ring_send.at[1, s], ring_recv.at[1, s], below) for s in range(3)]
    got_up = [copy(of(z - s - 1), of(z - s - 1), ring_send.at[0, s], ring_recv.at[0, s], above) for s in range(4)]
    got_down = [copy(of(z + s + 1), of(z + s + 1), ring_send.at[1, s], ring_recv.at[1, s], below) for s in range(3)]
    ring_up[0].start()
    ring_down[0].start()
    for one in coef_out:
        one.start()

    for n in range(GROUP):
        got = copy(part, top_a.at[n], a_send.at[0], a_recv.at[n], sibling)
        pl.when(jnp.logical_or(inner == 0, r != n))(got.wait_recv)

    @pl.when(inner == 1)
    def _():
        top_a[r] = part[...]

    total = (top_a[0].astype(F32) + top_a[1].astype(F32)) + (top_a[2].astype(F32) + top_a[3].astype(F32))
    coef_top[...] = total.astype(BF16)
    to_peers = []
    for device, jj, xo in peers:
        slot = 4 * ((jj + odd) % 2) + (4 - xo) % 4
        one = copy(coef_top, top_b.at[slot, sum_of], b_send.at[4 * jj + xo], b_recv.at[slot], (device, c))
        to_peers.append(one)
        if_not(odd == 0, jj == 0 and xo == 0, one.start)

    @pl.when(r == 0)
    def _():
        top_b[0, sum_of] = coef_top[...]

    got_up[0].wait_recv()
    ring_up[1].start()
    got_down[0].wait_recv()
    ring_down[1].start()
    forward(0)

    loads[4].wait()
    loads[8].wait()
    for one in coef_out:
        one.wait_recv()

    def far_step(i):
        picked = [coef[jnp.clip(leaf_far[f, i] - (d * OWN - HALO), 0, WINDOW - 1)] for f in range(4)]
        lfield[i] = dot(cpl[i], jnp.concatenate(picked, axis=0))

    by_fours(far_step)
    got_up[1].wait_recv()
    ring_up[2].start()
    got_down[1].wait_recv()
    ring_down[2].start()

    for n in range(8):
        loads[10 + n].wait()
    for n in range(8):
        got = copy(coef_top, top_b.at[n, sum_of], b_send.at[n], b_recv.at[n], sibling)
        if_not(odd == 0, n == 0, got.wait_recv)
    terms = [dot(top[n], top_b[n].reshape(2 * RANK, HALF)) for n in range(8)]
    total = ((terms[0] + terms[1]) + (terms[2] + terms[3])) + ((terms[4] + terms[5]) + (terms[6] + terms[7]))
    field[...] = total.astype(BF16)
    fields_out = [copy(field, top_c.at[o], c_send.at[o], c_recv.at[o], mates[o]) for o in range(3)]
    for one in fields_out:
        one.start()
    got_up[2].wait_recv()
    ring_up[3].start()
    got_down[2].wait_recv()
    forward(1)
    got_up[3].wait_recv()

    theirs = mid.at[pl.ds(base + (1 - half) * base, base)]
    there = mid.at[pl.ds(3 * base * half, base)]
    cross = copy(
        theirs, mid.at[pl.ds(3 * base * half, base)], ring_send.at[1, 3], ring_recv.at[1, 3], across
    )
    cross.start()
    for one in fields_out:
        one.wait_recv()
    top_field = ((total + top_c[0].astype(F32)) + (top_c[1].astype(F32) + top_c[2].astype(F32))).astype(BF16)
    lifted = [dot_t(upm[q], top_field) for q in range(MIDS)]
    forward(2)

    loads[5].wait()
    loads[9].wait()
    copy(theirs, there, ring_send.at[1, 3], ring_recv.at[1, 3], across).wait_recv()
    first = column * RING * MIDS - base
    for q in range(MIDS):
        picked = [mid[jnp.clip(mid_far[q, f] - first, 0, MID_WINDOW - 1)] for f in range(4)]
        value = (dot(mcp[q], jnp.concatenate(picked, axis=0)) + lifted[q]).astype(BF16)
        down = dot_t(upl[q], value).reshape(8, RANK, HALF)
        lfield[pl.ds(8 * q, 8)] = lfield[pl.ds(8 * q, 8)] + down
    forward(3)

    loads[6].wait()
    loads[7].wait()
    to_sibling.wait_recv()
    for i in range(CHUNKS):
        fwd_low[i].wait_recv()
        fwd_high[i].wait_recv()
    for load in tile_loads:
        load.wait()

    def give_copy(i):
        return copy(give.at[i], take.at[i], give_send.at[i], give_recv.at[i], sibling)

    def near_leaf(i):
        terms = []
        for s in range(SLOTS):
            slot = c * SLOTS + s
            j = jnp.clip(near_index[slot, i] - (d * OWN - HALO), 0, WINDOW - 1)
            j = jnp.where(slot < near_count[i], j, WINDOW)
            terms.append(dot(tile[i, s], jnp.concatenate([w0[j], w1[j]], axis=1)))
        total = (terms[0] + terms[1]) + (terms[2] + terms[3])
        give[i] = total[:, HALF:].astype(BF16)
        give_copy(i).start()
        near[i] = total[:, :HALF] + dot_t(bas[i], lfield[i].astype(BF16))

    def near_step(k, _):
        near_leaf(2 * k)
        near_leaf(2 * k + 1)
        return 0

    lax.fori_loop(0, OWN // 2, near_step, 0)

    def drain(i, _):
        give_copy(i).wait()
        return 0

    lax.fori_loop(0, OWN, drain, 0)
    to_sibling.wait_send()
    for one in to_after + to_before + fwd_low + fwd_high + coef_out + ring_up + ring_down + [cross] + fields_out:
        one.wait_send()
    for n in range(4):
        if_not(r == n + 1, n < 2, sums_out[n].wait_send)
    for n in range(8):
        if_not(odd == 0, n == 0, to_peers[n].wait_send)


def shards(
    sources, near_tiles, near_index, near_count, leaf_basis, leaf_coupling, leaf_far, up_leaf, mid_coupling, mid_far,
    up_mid, top_coupling,
):
    hbm_spec = pl.BlockSpec(memory_space=pltpu.MemorySpace.HBM)
    vmem_spec = pl.BlockSpec(memory_space=pltpu.MemorySpace.VMEM)
    dma, vmem, smem = pltpu.SemaphoreType.DMA, pltpu.VMEM, pltpu.SMEM
    operands = [
        sources.reshape(OWN, LEAF, HALF), near_tiles, near_index.T, near_count, leaf_basis, leaf_coupling, leaf_far.T,
        up_leaf, mid_coupling, mid_far, up_mid, top_coupling,
    ]
    near, take = pl.pallas_call(
        kernel,
        out_shape=(
            jax.ShapeDtypeStruct((OWN, LEAF, HALF), F32),
            jax.ShapeDtypeStruct((OWN, LEAF, HALF), BF16),
        ),
        in_specs=[hbm_spec] * 12,
        out_specs=(vmem_spec, vmem_spec),
        scratch_shapes=[
            smem((2 * SLOTS, OWN), jnp.int32), smem((OWN,), jnp.int32),
            smem((4, OWN), jnp.int32), smem((MIDS, 4), jnp.int32),
            vmem((WINDOW + 1, LEAF, HALF), BF16),
            vmem((WINDOW + 1, LEAF, HALF), BF16),
            vmem((OWN, SLOTS, LEAF, LEAF), BF16),
            vmem((OWN, RANK, LEAF), BF16),
            vmem((OWN, RANK, 4 * RANK), BF16),
            vmem((MIDS, RANK, 8 * RANK), BF16),
            vmem((MIDS, RANK, 4 * RANK), BF16),
            vmem((MIDS, RANK, RANK), BF16),
            vmem((8, RANK, 2 * RANK), BF16),
            vmem((WINDOW, RANK, HALF), BF16),
            vmem((MID_WINDOW, RANK, HALF), BF16),
            vmem((RANK, HALF), BF16),
            vmem((GROUP, RANK, HALF), BF16),
            vmem((RANK, HALF), BF16),
            vmem((8, 2, RANK, HALF), BF16),
            vmem((RANK, HALF), BF16),
            vmem((3, RANK, HALF), BF16),
            vmem((OWN, RANK, HALF), F32),
            vmem((OWN, LEAF, HALF), BF16),
            dma((18,)), dma((4,)),
            dma(()), dma(()),
            dma((2, CHUNKS)), dma((2, CHUNKS)),
            dma((2, CHUNKS)), dma((2, CHUNKS)),
            dma((2,)), dma((2,)),
            dma((2, 4)), dma((2, 4)),
            dma((4,)), dma((GROUP,)),
            dma((8,)), dma((8,)),
            dma((3,)), dma((3,)),
            dma((OWN,)), dma((OWN,)),
        ],
        compiler_params=pltpu.CompilerParams(
            collective_id=0, has_side_effects=True, vmem_limit_bytes=48 * 2**20
        ),
        name="h2_product",
    )(*[pltpu.with_memory_space_constraint(v, pltpu.MemorySpace.HBM) for v in operands])
    return (near + take.astype(F32)).reshape(OWN * LEAF, HALF)


def solution(mesh):
    return jax.shard_map(
        shards,
        mesh=mesh,
        in_specs=(
            P("leaf", "col"),
            P("leaf", "col", None, None),
            P("leaf", None),
            P("leaf"),
            P("leaf", None, None),
            P("leaf", None, None),
            P("leaf", None),
            P("leaf", None, None),
            P("leaf", None, None),
            P("leaf", None),
            P("leaf", None, None),
            P(),
        ),
        out_specs=P("leaf", "col"),
        check_vma=False,
    )
```

time: 71.6 us -> 57.9 us (0.81)
  the two profiles are of different devices: /device:TPU:4 before, /device:TPU:1 now
where the time goes in v2:
time: 57.9 us; the launch traced here: 57 us
  Pallas kernels  55.4 us (96%)
  other arithmetic  1.53 us (3%)
    pallas_call x1, Pallas kernels, shards(): pl.pallas_call(kernel, out_shape=(jax.ShapeDtypeStruct((OWN, LEAF, HALF),...  55.4 us
    add x1, other arithmetic, shards(): return (near + take.astype(F32)).reshape(OWN * LEAF, HALF)  1.53 us

profile of v2, /device:TPU:1, one launch (start us, length us, event | category | flops | bytes accessed | tf_op | source)
XLA Modules:
  0.0 57.0 jit_solution(7355872760448023054)
XLA Ops:
  0.0 55.4 %h2_product.1 = (f32[16,256,128]{2,1,0:T(8,128)S(1)}, bf16[16,256,128]{2,1,0:T(8,128)(2,1)S(1)}) custom-call(bf16[16,256,128]{2,1,0:T(8,128)(2,1)} %bitcast.4, bf16[16,4,256,256]{3,2,1,0:T(8,128)(2,1)} %tiles.1, s32[8,16]{1,0:T(8,128)} %bitcast.5, s32[16]{0:T(128)} %near_count_in.1, bf16[16,64,256]{2,1,0:T(8,128)(2,1)} %basis.1, ...), custom_call_target="tpu_custom_call" | custom-call | tf_op jit(solution)/shard_map/h2_product/pallas_call | solution.py:343
  55.4 1.5 %convert_add_fusion = f32[16,256,128]{2,1,0:T(8,128)} fusion(f32[16,256,128]{2,1,0:T(8,128)S(1)} %get-tuple-element.7, bf16[16,256,128]{2,1,0:T(8,128)(2,1)S(1)} %get-tuple-element.8), kind=kLoop, calls=%fused_computation | loop fusion | flops 1048576 | bytes 5242880 | tf_op jit(solution)/shard_map/add | solution.py:389

commit v3 on v2

--- a/solution.py
+++ b/solution.py
@@ -22,17 +22,12 @@
 COLUMNS = 16
 SLOTS = 4
 WINDOW = OWN + 2 * HALO
-CHUNK = 2
-CHUNKS = HALO // CHUNK
+CHUNKS = (4, 2, 2)
 MID_WINDOW = 4 * GROUP * MIDS
 
 
 def dot(a, b):
     return jnp.dot(a, b, preferred_element_type=F32)
-
-
-def dot_t(a, b):
-    return lax.dot_general(a, b, (((0,), (0,)), ((), ())), preferred_element_type=F32)
 
 
 def by_fours(body):
@@ -49,9 +44,9 @@
     top_coupling,
     near, take,
     near_index, near_count, leaf_far, mid_far,
-    w0, w1, tile, bas, cpl, upl, mcp, upm, top, coef, mid, part, top_a, coef_top, top_b, field, top_c, lfield, give,
+    own0, own1, ha0, ha1, hb0, hb1, hc0, hc1, tile, bas, cpl, upl, mcp, upm, bat, upl_t, upm_t, top, coef, mid, part, top_a, coef_top, top_b, field, top_c, lfield, give,
     load_sem, tile_sem, sib_send, sib_recv, halo_send, halo_recv, fwd_send, fwd_recv, coef_send, coef_recv,
-    ring_send, ring_recv, a_send, a_recv, b_send, b_recv, c_send, c_recv, give_send, give_recv,
+    mid_send, mid_recv, cross_send, cross_recv, a_send, a_recv, b_send, b_recv, c_send, c_recv, give_send, give_recv,
 ):
     d, c = lax.axis_index("leaf"), lax.axis_index("col")
     devices = COLUMNS * RING
@@ -60,7 +55,6 @@
     half, x, y = g % 2, column % 4, column // 4
     sibling = (d, 1 - c)
     after, before = ((d + 1) % devices, c), ((d + devices - 1) % devices, c)
-    above, below = (column * RING + (z + 1) % RING, c), (column * RING + (z + RING - 1) % RING, c)
     mates = [(g * GROUP + (r + o) % GROUP, c) for o in (1, 2, 3)]
     inner = (r * (3 - r)) // 2
     other = column * RING + (1 - half) * GROUP
@@ -96,7 +90,7 @@
         if_not(odd == 0, jj == 0 and xo == 0, functools.partial(greet, (device, c)))
 
     loads = [
-        pltpu.make_async_copy(src, w0.at[pl.ds(HALO, OWN)], load_sem.at[0]),
+        pltpu.make_async_copy(src, own0.at[pl.ds(0, OWN)], load_sem.at[0]),
         pltpu.make_async_copy(basis, bas, load_sem.at[1]),
         pltpu.make_async_copy(up_leaf, upl, load_sem.at[2]),
         pltpu.make_async_copy(up_mid, upm, load_sem.at[3]),
@@ -125,8 +119,8 @@
         load.start()
 
     zero = jnp.zeros((LEAF, HALF), BF16)
-    w0[WINDOW] = zero
-    w1[WINDOW] = zero
+    own0[OWN] = zero
+    own1[OWN] = zero
     for n in range(8):
         top_b[n, 1 - sum_of] = jnp.zeros((RANK, HALF), BF16)
 
@@ -139,36 +133,34 @@
     def _():
         pl.semaphore_wait(barrier, 20)
 
-    to_sibling = copy(src, w1.at[pl.ds(HALO, OWN)], sib_send, sib_recv, sibling)
-    to_after, to_before, fwd_low, fwd_high = [], [], [], []
-    for i in range(CHUNKS):
-        low = pl.ds(HALO - CHUNK * (i + 1), CHUNK)
-        high = pl.ds(HALO + OWN + CHUNK * i, CHUNK)
-        to_after.append(
-            copy(src.at[pl.ds(OWN - CHUNK * (i + 1), CHUNK)], w0.at[low], halo_send.at[0, i], halo_recv.at[0, i], after)
+    to_sibling = copy(src, own1.at[pl.ds(0, OWN)], sib_send, sib_recv, sibling)
+    halos, forwards = [], []
+    done = 0
+    for i, (h0, h1) in enumerate(((ha0, ha1), (hb0, hb1), (hc0, hc1))):
+        n = CHUNKS[i]
+        halos.append(
+            (
+                copy(src.at[pl.ds(OWN - done - n, n)], h0.at[0], halo_send.at[0, i], halo_recv.at[0, i], after),
+                copy(src.at[pl.ds(done, n)], h0.at[1], halo_send.at[1, i], halo_recv.at[1, i], before),
+            )
         )
-        to_before.append(
-            copy(src.at[pl.ds(CHUNK * i, CHUNK)], w0.at[high], halo_send.at[1, i], halo_recv.at[1, i], before)
-        )
-        fwd_low.append(copy(w0.at[low], w1.at[low], fwd_send.at[0, i], fwd_recv.at[0, i], sibling))
-        fwd_high.append(copy(w0.at[high], w1.at[high], fwd_send.at[1, i], fwd_recv.at[1, i], sibling))
+        forwards.append(copy(h0, h1, fwd_send.at[i], fwd_recv.at[i], sibling))
+        done += n
 
     def forward(i):
-        to_after[i].wait_recv()
-        to_before[i].wait_recv()
-        fwd_low[i].start()
-        fwd_high[i].start()
-
-    for i in range(CHUNKS):
-        to_after[i].start()
-        to_before[i].start()
+        for one in halos[i]:
+            one.wait_recv()
+        forwards[i].start()
+
+    for one in halos[0]:
+        one.start()
     to_sibling.start()
 
     loads[0].wait()
     loads[1].wait()
 
     def leaf_step(i):
-        coef[HALO + i] = dot(bas[i], w0[HALO + i]).astype(BF16)
+        coef[HALO + i] = dot(bas[i], own0[i]).astype(BF16)
 
     by_fours(leaf_step)
     coef_out = [
@@ -190,15 +182,33 @@
     for n in range(4):
         if_not(r == n + 1, n < 2, sums_out[n].start)
 
-    def of(origin):
-        return mid.at[pl.ds(base + MIDS * ((origin + RING) % RING), MIDS)]
-
-    ring_up = [copy(of(z - s), of(z - s), ring_send.at[0, s], ring_recv.at[0, s], above) for s in range(4)]
-    ring_down = [copy(of(z + s), of(z + s), ring_send.at[1, s], ring_recv.at[1, s], below) for s in range(3)]
-    got_up = [copy(of(z - s - 1), of(z - s - 1), ring_send.at[0, s], ring_recv.at[0, s], above) for s in range(4)]
-    got_down = [copy(of(z + s + 1), of(z + s + 1), ring_send.at[1, s], ring_recv.at[1, s], below) for s in range(3)]
-    ring_up[0].start()
-    ring_down[0].start()
+    def near_z(o):
+        return (column * RING + (z + o + RING) % RING, c)
+
+    def of(o):
+        return mid.at[pl.ds(base + MIDS * ((z + o + RING) % RING), MIDS)]
+
+    up = 1 - 2 * c
+    steps = [(0, 1), (0, -1), (0, 2), (0, -2), (-2, 1), (2, -1), (-2 * up, 2 * up)]
+    mid_out = [
+        copy(of(whose), of(whose), mid_send.at[n], mid_recv.at[n], near_z(o)) for n, (whose, o) in enumerate(steps)
+    ]
+    mid_got = [
+        copy(of(whose - o), of(whose - o), mid_send.at[n], mid_recv.at[n], near_z(o))
+        for n, (whose, o) in enumerate(steps)
+    ]
+
+    def cross(o):
+        member = (z + o + RING) % GROUP
+        there = mid.at[pl.ds(3 * base * half + MIDS * member, MIDS)]
+        return copy(of(o), there, cross_send.at[member], cross_recv.at[member], across)
+
+    def send_across(offsets):
+        for o in offsets:
+            pl.when(((z + o + RING) % RING) // GROUP != half)(cross(o).start)
+
+    for n in range(4):
+        mid_out[n].start()
     for one in coef_out:
         one.start()
 
@@ -219,16 +229,28 @@
         to_peers.append(one)
         if_not(odd == 0, jj == 0 and xo == 0, one.start)
 
+    for one in halos[1]:
+        one.start()
+
     @pl.when(r == 0)
     def _():
         top_b[0, sum_of] = coef_top[...]
 
-    got_up[0].wait_recv()
-    ring_up[1].start()
-    got_down[0].wait_recv()
-    ring_down[1].start()
-    forward(0)
-
+    for n in (2, 3):
+        mid_got[n].wait_recv()
+    for n in (4, 5, 6):
+        mid_out[n].start()
+    for n in (0, 1):
+        mid_got[n].wait_recv()
+    send_across((1, -1, 2, -2))
+
+    def turn(i):
+        bat[i] = bas[i].T
+
+    by_fours(turn)
+    for q in range(MIDS):
+        upl_t[q] = upl[q].T
+        upm_t[q] = upm[q].T
     loads[4].wait()
     loads[8].wait()
     for one in coef_out:
@@ -239,10 +261,6 @@
         lfield[i] = dot(cpl[i], jnp.concatenate(picked, axis=0))
 
     by_fours(far_step)
-    got_up[1].wait_recv()
-    ring_up[2].start()
-    got_down[1].wait_recv()
-    ring_down[2].start()
 
     for n in range(8):
         loads[10 + n].wait()
@@ -255,76 +273,99 @@
     fields_out = [copy(field, top_c.at[o], c_send.at[o], c_recv.at[o], mates[o]) for o in range(3)]
     for one in fields_out:
         one.start()
-    got_up[2].wait_recv()
-    ring_up[3].start()
-    got_down[2].wait_recv()
-    forward(1)
-    got_up[3].wait_recv()
-
-    theirs = mid.at[pl.ds(base + (1 - half) * base, base)]
-    there = mid.at[pl.ds(3 * base * half, base)]
-    cross = copy(
-        theirs, mid.at[pl.ds(3 * base * half, base)], ring_send.at[1, 3], ring_recv.at[1, 3], across
-    )
-    cross.start()
+    for one in halos[2]:
+        one.start()
+    for n in (4, 5, 6):
+        mid_got[n].wait_recv()
+    send_across((3, -3, 4))
+
+    reach = [(ha0, ha1, 4, 20), (hb0, hb1, 2, 26), (hc0, hc1, 0, 30)]
+    batches = [(4, 4, 4), (2, 10, 2), (0, 14, 2)]
+
+    def give_copy(phase, k):
+        first, step, n = batches[phase]
+        here = pl.ds(first + step * k, n)
+        return copy(give.at[here], take.at[here], give_send.at[phase, k], give_recv.at[phase, k], sibling)
+
+    def near_rows(i, s, k, phase):
+        slot = c * SLOTS + s
+        j = near_index[slot, i] - (d * OWN - HALO)
+        live = slot < near_count[i]
+        inside = jnp.logical_and(live, jnp.logical_and(j >= HALO, j < HALO + OWN))
+        m = jnp.where(inside, jnp.clip(j - HALO, 0, OWN - 1), OWN)
+        low, high = own0[m], own1[m]
+        for p in range(phase + 1):
+            h0, h1, first, step = reach[p]
+            m = j - (first + step * k)
+            inside = jnp.logical_and(live, jnp.logical_and(m >= 0, m < CHUNKS[p]))
+            m = jnp.clip(m, 0, CHUNKS[p] - 1)
+            low, high = jnp.where(inside, h0[k, m], low), jnp.where(inside, h1[k, m], high)
+        return jnp.concatenate([low, high], axis=1)
+
+    def near_phase(phase, fresh=False):
+        forwards[phase].wait_recv()
+        first, step, n = batches[phase]
+
+        def side(k, _):
+            for i in range(n):
+                leaf = first + step * k + i
+                terms = [dot(tile[leaf, s], near_rows(leaf, s, k, phase)) for s in range(SLOTS)]
+                total = (terms[0] + terms[1]) + (terms[2] + terms[3])
+                give[leaf] = total[:, HALF:].astype(BF16)
+                near[leaf] = total[:, :HALF] if fresh else near[leaf] + total[:, :HALF]
+            give_copy(phase, k).start()
+            return 0
+
+        lax.fori_loop(0, 2, side, 0)
+
+    loads[6].wait()
+    loads[7].wait()
+    to_sibling.wait_recv()
+    for load in tile_loads:
+        load.wait()
+
+    forward(0)
+    near_phase(0, True)
     for one in fields_out:
         one.wait_recv()
     top_field = ((total + top_c[0].astype(F32)) + (top_c[1].astype(F32) + top_c[2].astype(F32))).astype(BF16)
-    lifted = [dot_t(upm[q], top_field) for q in range(MIDS)]
-    forward(2)
+    lifted = [dot(upm_t[q], top_field) for q in range(MIDS)]
 
     loads[5].wait()
     loads[9].wait()
-    copy(theirs, there, ring_send.at[1, 3], ring_recv.at[1, 3], across).wait_recv()
+    for n in range(GROUP):
+        got = mid.at[pl.ds(3 * base * half + MIDS * n, MIDS)]
+        copy(got, got, cross_send.at[n], cross_recv.at[n], across).wait_recv()
     first = column * RING * MIDS - base
     for q in range(MIDS):
         picked = [mid[jnp.clip(mid_far[q, f] - first, 0, MID_WINDOW - 1)] for f in range(4)]
         value = (dot(mcp[q], jnp.concatenate(picked, axis=0)) + lifted[q]).astype(BF16)
-        down = dot_t(upl[q], value).reshape(8, RANK, HALF)
+        down = dot(upl_t[q], value).reshape(8, RANK, HALF)
         lfield[pl.ds(8 * q, 8)] = lfield[pl.ds(8 * q, 8)] + down
-    forward(3)
-
-    loads[6].wait()
-    loads[7].wait()
-    to_sibling.wait_recv()
-    for i in range(CHUNKS):
-        fwd_low[i].wait_recv()
-        fwd_high[i].wait_recv()
-    for load in tile_loads:
-        load.wait()
-
-    def give_copy(i):
-        return copy(give.at[i], take.at[i], give_send.at[i], give_recv.at[i], sibling)
-
-    def near_leaf(i):
-        terms = []
-        for s in range(SLOTS):
-            slot = c * SLOTS + s
-            j = jnp.clip(near_index[slot, i] - (d * OWN - HALO), 0, WINDOW - 1)
-            j = jnp.where(slot < near_count[i], j, WINDOW)
-            terms.append(dot(tile[i, s], jnp.concatenate([w0[j], w1[j]], axis=1)))
-        total = (terms[0] + terms[1]) + (terms[2] + terms[3])
-        give[i] = total[:, HALF:].astype(BF16)
-        give_copy(i).start()
-        near[i] = total[:, :HALF] + dot_t(bas[i], lfield[i].astype(BF16))
-
-    def near_step(k, _):
-        near_leaf(2 * k)
-        near_leaf(2 * k + 1)
+
+    def product_step(k, _):
+        for i in range(4):
+            inner_leaf, outer_leaf = 4 + 4 * k + i, 12 * k + i
+            near[inner_leaf] = near[inner_leaf] + dot(bat[inner_leaf], lfield[inner_leaf].astype(BF16))
+            near[outer_leaf] = dot(bat[outer_leaf], lfield[outer_leaf].astype(BF16))
         return 0
 
-    lax.fori_loop(0, OWN // 2, near_step, 0)
-
-    def drain(i, _):
-        give_copy(i).wait()
-        return 0
-
-    lax.fori_loop(0, OWN, drain, 0)
+    lax.fori_loop(0, 2, product_step, 0)
+
+    forward(1)
+    forward(2)
+    near_phase(1)
+    near_phase(2)
+
+    for phase in range(3):
+        for k in range(2):
+            give_copy(phase, k).wait()
     to_sibling.wait_send()
-    for one in to_after + to_before + fwd_low + fwd_high + coef_out + ring_up + ring_down + [cross] + fields_out:
+    for one in [one for pair in halos for one in pair] + forwards + coef_out + mid_out + fields_out:
         one.wait_send()
-    for n in range(4):
+    for n in range(GROUP):
         if_not(r == n + 1, n < 2, sums_out[n].wait_send)
+        cross(4 - r + n).wait_send()
     for n in range(8):
         if_not(odd == 0, n == 0, to_peers[n].wait_send)
 
@@ -351,13 +392,17 @@
         scratch_shapes=[
             smem((2 * SLOTS, OWN), jnp.int32), smem((OWN,), jnp.int32),
             smem((4, OWN), jnp.int32), smem((MIDS, 4), jnp.int32),
-            vmem((WINDOW + 1, LEAF, HALF), BF16),
-            vmem((WINDOW + 1, LEAF, HALF), BF16),
+            vmem((OWN + 1, LEAF, HALF), BF16),
+            vmem((OWN + 1, LEAF, HALF), BF16),
+            *[vmem((2, n, LEAF, HALF), BF16) for n in CHUNKS for _ in range(2)],
             vmem((OWN, SLOTS, LEAF, LEAF), BF16),
             vmem((OWN, RANK, LEAF), BF16),
             vmem((OWN, RANK, 4 * RANK), BF16),
             vmem((MIDS, RANK, 8 * RANK), BF16),
             vmem((MIDS, RANK, 4 * RANK), BF16),
+            vmem((MIDS, RANK, RANK), BF16),
+            vmem((OWN, LEAF, RANK), BF16),
+            vmem((MIDS, 8 * RANK, RANK), BF16),
             vmem((MIDS, RANK, RANK), BF16),
             vmem((8, RANK, 2 * RANK), BF16),
             vmem((WINDOW, RANK, HALF), BF16),
@@ -372,14 +417,15 @@
             vmem((OWN, LEAF, HALF), BF16),
             dma((18,)), dma((4,)),
             dma(()), dma(()),
-            dma((2, CHUNKS)), dma((2, CHUNKS)),
-            dma((2, CHUNKS)), dma((2, CHUNKS)),
+            dma((2, 3)), dma((2, 3)),
+            dma((3,)), dma((3,)),
             dma((2,)), dma((2,)),
-            dma((2, 4)), dma((2, 4)),
+            dma((7,)), dma((7,)),
+            dma((GROUP,)), dma((GROUP,)),
             dma((4,)), dma((GROUP,)),
             dma((8,)), dma((8,)),
             dma((3,)), dma((3,)),
-            dma((OWN,)), dma((OWN,)),
+            dma((3, 2)), dma((3, 2)),
         ],
         compiler_params=pltpu.CompilerParams(
             collective_id=0, has_side_effects=True, vmem_limit_bytes=48 * 2**20

time: 57.9 us -> 44.8 us (0.77); the launches traced: 57 us -> 44.8 us
  Pallas kernels: 55.4 us -> 43.2 us
    pallas_call x1, Pallas kernels: 55.4 us -> 43.2 us  [shards(): pl.pallas_call(kernel, out_shape=(jax.ShapeDtypeStruct((OWN, LEAF, HALF),...]
where the time goes in v3:
time: 44.8 us
  Pallas kernels  43.2 us (96%)
  other arithmetic  1.53 us (3%)
    pallas_call x1, Pallas kernels, shards(): pl.pallas_call(kernel, out_shape=(jax.ShapeDtypeStruct((OWN, LEAF, HALF),...  43.2 us
    add x1, other arithmetic, shards(): return (near + take.astype(F32)).reshape(OWN * LEAF, HALF)  1.53 us

profile of v3, /device:TPU:1, one launch (start us, length us, event | category | flops | bytes accessed | tf_op | source)
XLA Modules:
  0.0 44.8 jit_solution(579696191729633320)
XLA Ops:
  0.0 43.2 %h2_product.1 = (f32[16,256,128]{2,1,0:T(8,128)S(1)}, bf16[16,256,128]{2,1,0:T(8,128)(2,1)S(1)}) custom-call(bf16[16,256,128]{2,1,0:T(8,128)(2,1)} %bitcast.4, bf16[16,4,256,256]{3,2,1,0:T(8,128)(2,1)} %tiles.1, s32[8,16]{1,0:T(8,128)} %bitcast.5, s32[16]{0:T(128)} %near_count_in.1, bf16[16,64,256]{2,1,0:T(8,128)(2,1)} %basis.1, ...), custom_call_target="tpu_custom_call" | custom-call | tf_op jit(solution)/shard_map/h2_product/pallas_call | solution.py:384
  43.2 1.5 %convert_add_fusion = f32[16,256,128]{2,1,0:T(8,128)} fusion(f32[16,256,128]{2,1,0:T(8,128)S(1)} %get-tuple-element.7, bf16[16,256,128]{2,1,0:T(8,128)(2,1)S(1)} %get-tuple-element.8), kind=kLoop, calls=%fused_computation | loop fusion | flops 1048576 | bytes 5242880 | tf_op jit(solution)/shard_map/add | solution.py:435

commit v4 on v3

--- a/solution.py
+++ b/solution.py
@@ -1,5 +1,3 @@
-import functools
-
 import jax
 import jax.numpy as jnp
 from jax import lax
@@ -22,7 +20,9 @@
 COLUMNS = 16
 SLOTS = 4
 WINDOW = OWN + 2 * HALO
-CHUNKS = (4, 2, 2)
+CHUNKS = (2, 2, 2, 2)
+TOP_WIDTH = 2 * COLUMNS * RANK
+ROWS = 2 * RANK // RING
 MID_WINDOW = 4 * GROUP * MIDS
 
 
@@ -44,9 +44,9 @@
     top_coupling,
     near, take,
     near_index, near_count, leaf_far, mid_far,
-    own0, own1, ha0, ha1, hb0, hb1, hc0, hc1, tile, bas, cpl, upl, mcp, upm, bat, upl_t, upm_t, top, coef, mid, part, top_a, coef_top, top_b, field, top_c, lfield, give,
+    own0, own1, ha0, ha1, hb0, hb1, hc0, hc1, hd0, hd1, tile, bas, cpl, upl, mcp, upm, bat, upl_t, upm_t, top, coef, mid, part, top_b, field, top_c, rows, lfield, give,
     load_sem, tile_sem, sib_send, sib_recv, halo_send, halo_recv, fwd_send, fwd_recv, coef_send, coef_recv,
-    mid_send, mid_recv, cross_send, cross_recv, a_send, a_recv, b_send, b_recv, c_send, c_recv, give_send, give_recv,
+    mid_send, mid_recv, cross_send, cross_recv, b_send, b_recv, c_send, c_recv, d_send, d_recv, give_send, give_recv,
 ):
     d, c = lax.axis_index("leaf"), lax.axis_index("col")
     devices = COLUMNS * RING
@@ -56,14 +56,8 @@
     sibling = (d, 1 - c)
     after, before = ((d + 1) % devices, c), ((d + devices - 1) % devices, c)
     mates = [(g * GROUP + (r + o) % GROUP, c) for o in (1, 2, 3)]
-    inner = (r * (3 - r)) // 2
-    other = column * RING + (1 - half) * GROUP
-    sums = [(g * GROUP + 1, c), (g * GROUP + 2, c), (other, c), (other + 3, c)]
-    sum_of = inner * half + (1 - inner) * (1 - half)
-    odd = r // 2
-    peers = [
-        (((((y + 2 * jj + odd) % 4) * 4 + (x + xo) % 4) * RING + z), jj, xo) for jj in range(2) for xo in range(4)
-    ]
+    offsets = [(yo, xo) for yo in range(4) for xo in range(4) if yo or xo]
+    peers = [((((y + yo) % 4) * 4 + (x + xo) % 4) * RING + z, c) for yo, xo in offsets]
     across = (((column + 1 - 2 * half + COLUMNS) % COLUMNS) * RING + z, c)
     across_from = (((column - 1 + 2 * half + COLUMNS) % COLUMNS) * RING + z, c)
 
@@ -72,22 +66,15 @@
             src_ref=a, dst_ref=b, send_sem=send, recv_sem=recv, device_id=device, device_id_type=MESH
         )
 
-    def if_not(flag, here, body):
-        if here:
-            pl.when(jnp.logical_not(flag))(body)
-        else:
-            body()
-
     barrier = pltpu.get_barrier_semaphore()
 
     def greet(device):
         pl.semaphore_signal(barrier, inc=1, device_id=device, device_id_type=MESH)
 
     column_mates = [(column * RING + (z + o) % RING, c) for o in range(1, RING)]
-    for device in [sibling, after, before, across, across_from] + column_mates:
+    greeted = [sibling, after, before, across, across_from] + column_mates + peers
+    for device in greeted:
         greet(device)
-    for device, jj, xo in peers:
-        if_not(odd == 0, jj == 0 and xo == 0, functools.partial(greet, (device, c)))
 
     loads = [
         pltpu.make_async_copy(src, own0.at[pl.ds(0, OWN)], load_sem.at[0]),
@@ -101,15 +88,7 @@
         pltpu.make_async_copy(coupling, cpl, load_sem.at[8]),
         pltpu.make_async_copy(mid_coupling, mcp, load_sem.at[9]),
     ]
-    for device, jj, xo in peers:
-        pair = ((y + 2 * jj + odd) % 4) * 4 + (x + xo) % 4
-        loads.append(
-            pltpu.make_async_copy(
-                top_coupling.at[g, :, pl.ds(pl.multiple_of(pair * 2 * RANK, 2 * RANK), 2 * RANK)],
-                top.at[4 * jj + xo],
-                load_sem.at[10 + 4 * jj + xo],
-            )
-        )
+    loads.append(pltpu.make_async_copy(top_coupling.at[pl.ds(2 * column, 2)], top, load_sem.at[10]))
     for load in loads:
         load.start()
     tile_loads = [
@@ -121,22 +100,14 @@
     zero = jnp.zeros((LEAF, HALF), BF16)
     own0[OWN] = zero
     own1[OWN] = zero
-    for n in range(8):
-        top_b[n, 1 - sum_of] = jnp.zeros((RANK, HALF), BF16)
-
-    @pl.when(odd == 0)
-    def _():
-        top_b[0, sum_of] = jnp.zeros((RANK, HALF), BF16)
-        pl.semaphore_wait(barrier, 19)
-
-    @pl.when(odd != 0)
-    def _():
-        pl.semaphore_wait(barrier, 20)
+    for n in range(COLUMNS):
+        top_b[n, 1 - half] = jnp.zeros((RANK, HALF), BF16)
+    pl.semaphore_wait(barrier, len(greeted))
 
     to_sibling = copy(src, own1.at[pl.ds(0, OWN)], sib_send, sib_recv, sibling)
     halos, forwards = [], []
     done = 0
-    for i, (h0, h1) in enumerate(((ha0, ha1), (hb0, hb1), (hc0, hc1))):
+    for i, (h0, h1) in enumerate(((ha0, ha1), (hb0, hb1), (hc0, hc1), (hd0, hd1))):
         n = CHUNKS[i]
         halos.append(
             (
@@ -178,9 +149,11 @@
     part[...] = (lifts[0] + lifts[1]).astype(BF16)
     for q in range(MIDS):
         mid[base + MIDS * z + q] = values[q]
-    sums_out = [copy(part, top_a.at[r], a_send.at[n], a_recv.at[r], sums[n]) for n in range(4)]
-    for n in range(4):
-        if_not(r == n + 1, n < 2, sums_out[n].start)
+
+    to_peers = []
+    for n, (yo, xo) in enumerate(offsets):
+        back = offsets.index(((4 - yo) % 4, (4 - xo) % 4))
+        to_peers.append(copy(part, top_b.at[column, half], b_send.at[n], b_recv.at[back], peers[n]))
 
     def near_z(o):
         return (column * RING + (z + o + RING) % RING, c)
@@ -209,33 +182,14 @@
 
     for n in range(4):
         mid_out[n].start()
+    for one in to_peers:
+        one.start()
     for one in coef_out:
         one.start()
-
-    for n in range(GROUP):
-        got = copy(part, top_a.at[n], a_send.at[0], a_recv.at[n], sibling)
-        pl.when(jnp.logical_or(inner == 0, r != n))(got.wait_recv)
-
-    @pl.when(inner == 1)
-    def _():
-        top_a[r] = part[...]
-
-    total = (top_a[0].astype(F32) + top_a[1].astype(F32)) + (top_a[2].astype(F32) + top_a[3].astype(F32))
-    coef_top[...] = total.astype(BF16)
-    to_peers = []
-    for device, jj, xo in peers:
-        slot = 4 * ((jj + odd) % 2) + (4 - xo) % 4
-        one = copy(coef_top, top_b.at[slot, sum_of], b_send.at[4 * jj + xo], b_recv.at[slot], (device, c))
-        to_peers.append(one)
-        if_not(odd == 0, jj == 0 and xo == 0, one.start)
+    top_b[column, half] = part[...]
 
     for one in halos[1]:
         one.start()
-
-    @pl.when(r == 0)
-    def _():
-        top_b[0, sum_of] = coef_top[...]
-
     for n in (2, 3):
         mid_got[n].wait_recv()
     for n in (4, 5, 6):
@@ -262,15 +216,23 @@
 
     by_fours(far_step)
 
-    for n in range(8):
-        loads[10 + n].wait()
-    for n in range(8):
-        got = copy(coef_top, top_b.at[n, sum_of], b_send.at[n], b_recv.at[n], sibling)
-        if_not(odd == 0, n == 0, got.wait_recv)
-    terms = [dot(top[n], top_b[n].reshape(2 * RANK, HALF)) for n in range(8)]
-    total = ((terms[0] + terms[1]) + (terms[2] + terms[3])) + ((terms[4] + terms[5]) + (terms[6] + terms[7]))
-    field[...] = total.astype(BF16)
-    fields_out = [copy(field, top_c.at[o], c_send.at[o], c_recv.at[o], mates[o]) for o in range(3)]
+    loads[10].wait()
+    lanes = pl.ds(pl.multiple_of(column * 2 * RANK, 2 * RANK), 2 * RANK)
+    itself = lax.broadcasted_iota(jnp.int32, (RANK, 2 * RANK), 1) // RANK == half
+    top[half, :, lanes] = jnp.where(itself, 0.0, top[half, :, lanes].astype(F32)).astype(BF16)
+
+    for n in range(len(peers)):
+        yo, xo = offsets[n]
+        from_column = ((y + yo) % 4) * 4 + (x + xo) % 4
+        copy(part, top_b.at[from_column, half], b_send.at[n], b_recv.at[n], sibling).wait_recv()
+    total = dot(top[...].reshape(2 * RANK, TOP_WIDTH), top_b[...].reshape(TOP_WIDTH, HALF))
+    field[...] = total.astype(BF16).reshape(RING, ROWS, HALF)
+    fields_out = []
+    for o in range(1, RING):
+        there = (z + o) % RING
+        fields_out.append(
+            copy(field.at[there], top_c.at[o], c_send.at[o - 1], c_recv.at[o - 1], column_mates[o - 1])
+        )
     for one in fields_out:
         one.start()
     for one in halos[2]:
@@ -278,9 +240,20 @@
     for n in (4, 5, 6):
         mid_got[n].wait_recv()
     send_across((3, -3, 4))
-
-    reach = [(ha0, ha1, 4, 20), (hb0, hb1, 2, 26), (hc0, hc1, 0, 30)]
-    batches = [(4, 4, 4), (2, 10, 2), (0, 14, 2)]
+    for one in fields_out:
+        one.wait_recv()
+    reduced = field[z].astype(F32)
+    for o in range(1, RING):
+        reduced = reduced + top_c[o].astype(F32)
+    rows[r] = reduced.astype(BF16)
+    rows_out = [copy(rows.at[r], rows.at[r], d_send.at[o], d_recv.at[o], mates[o]) for o in range(3)]
+    for one in rows_out:
+        one.start()
+    for one in halos[3]:
+        one.start()
+
+    reach = [(ha0, ha1, 6, 18), (hb0, hb1, 4, 22), (hc0, hc1, 2, 26), (hd0, hd1, 0, 30)]
+    batches = [(6, 2, 2), (4, 6, 2), (2, 10, 2), (0, 14, 2)]
 
     def give_copy(phase, k):
         first, step, n = batches[phase]
@@ -325,10 +298,13 @@
         load.wait()
 
     forward(0)
+    forward(1)
     near_phase(0, True)
-    for one in fields_out:
-        one.wait_recv()
-    top_field = ((total + top_c[0].astype(F32)) + (top_c[1].astype(F32) + top_c[2].astype(F32))).astype(BF16)
+    near_phase(1, True)
+    for n in range(3):
+        got = rows.at[(r + 3 - n) % GROUP]
+        copy(got, got, d_send.at[n], d_recv.at[n], sibling).wait_recv()
+    top_field = rows[...].reshape(RANK, HALF)
     lifted = [dot(upm_t[q], top_field) for q in range(MIDS)]
 
     loads[5].wait()
@@ -352,22 +328,19 @@
 
     lax.fori_loop(0, 2, product_step, 0)
 
-    forward(1)
     forward(2)
-    near_phase(1)
+    forward(3)
     near_phase(2)
-
-    for phase in range(3):
+    near_phase(3)
+
+    for phase in range(4):
         for k in range(2):
             give_copy(phase, k).wait()
     to_sibling.wait_send()
-    for one in [one for pair in halos for one in pair] + forwards + coef_out + mid_out + fields_out:
+    for one in [one for pair in halos for one in pair] + forwards + coef_out + mid_out + to_peers + fields_out + rows_out:
         one.wait_send()
     for n in range(GROUP):
-        if_not(r == n + 1, n < 2, sums_out[n].wait_send)
         cross(4 - r + n).wait_send()
-    for n in range(8):
-        if_not(odd == 0, n == 0, to_peers[n].wait_send)
 
 
 def shards(
@@ -404,28 +377,27 @@
             vmem((OWN, LEAF, RANK), BF16),
             vmem((MIDS, 8 * RANK, RANK), BF16),
             vmem((MIDS, RANK, RANK), BF16),
-            vmem((8, RANK, 2 * RANK), BF16),
+            vmem((2, RANK, TOP_WIDTH), BF16),
             vmem((WINDOW, RANK, HALF), BF16),
             vmem((MID_WINDOW, RANK, HALF), BF16),
             vmem((RANK, HALF), BF16),
-            vmem((GROUP, RANK, HALF), BF16),
-            vmem((RANK, HALF), BF16),
-            vmem((8, 2, RANK, HALF), BF16),
-            vmem((RANK, HALF), BF16),
-            vmem((3, RANK, HALF), BF16),
+            vmem((COLUMNS, 2, RANK, HALF), BF16),
+            vmem((RING, ROWS, HALF), BF16),
+            vmem((RING, ROWS, HALF), BF16),
+            vmem((GROUP, ROWS, HALF), BF16),
             vmem((OWN, RANK, HALF), F32),
             vmem((OWN, LEAF, HALF), BF16),
-            dma((18,)), dma((4,)),
+            dma((11,)), dma((4,)),
             dma(()), dma(()),
-            dma((2, 3)), dma((2, 3)),
-            dma((3,)), dma((3,)),
+            dma((2, 4)), dma((2, 4)),
+            dma((4,)), dma((4,)),
             dma((2,)), dma((2,)),
             dma((7,)), dma((7,)),
             dma((GROUP,)), dma((GROUP,)),
-            dma((4,)), dma((GROUP,)),
-            dma((8,)), dma((8,)),
+            dma((15,)), dma((15,)),
+            dma((7,)), dma((7,)),
             dma((3,)), dma((3,)),
-            dma((3, 2)), dma((3, 2)),
+            dma((4, 2)), dma((4, 2)),
         ],
         compiler_params=pltpu.CompilerParams(
             collective_id=0, has_side_effects=True, vmem_limit_bytes=48 * 2**20

time: 44.8 us -> 43.1 us (0.962)
  Pallas kernels: 43.2 us -> 41.1 us
    pallas_call x1, Pallas kernels: 43.2 us -> 41.1 us  [shards(): pl.pallas_call(kernel, out_shape=(jax.ShapeDtypeStruct((OWN, LEAF, HALF),...]
where the time goes in v4:
time: 43.1 us; the launch traced here: 42.7 us
  Pallas kernels  41.1 us (95%)
  other arithmetic  1.53 us (4%)
    pallas_call x1, Pallas kernels, shards(): pl.pallas_call(kernel, out_shape=(jax.ShapeDtypeStruct((OWN, LEAF, HALF),...  41.1 us
    add x1, other arithmetic, shards(): return (near + take.astype(F32)).reshape(OWN * LEAF, HALF)  1.53 us

profile of v4, /device:TPU:1, one launch (start us, length us, event | category | flops | bytes accessed | tf_op | source)
XLA Modules:
  0.0 42.7 jit_solution(11279517941474892639)
XLA Ops:
  0.0 41.1 %h2_product.1 = (f32[16,256,128]{2,1,0:T(8,128)S(1)}, bf16[16,256,128]{2,1,0:T(8,128)(2,1)S(1)}) custom-call(bf16[16,256,128]{2,1,0:T(8,128)(2,1)} %bitcast.4, bf16[16,4,256,256]{3,2,1,0:T(8,128)(2,1)} %tiles.1, s32[8,16]{1,0:T(8,128)} %bitcast.5, s32[16]{0:T(128)} %near_count_in.1, bf16[16,64,256]{2,1,0:T(8,128)(2,1)} %basis.1, ...), custom_call_target="tpu_custom_call" | custom-call | tf_op jit(solution)/shard_map/h2_product/pallas_call | solution.py:357
  41.1 1.5 %convert_add_fusion = f32[16,256,128]{2,1,0:T(8,128)} fusion(f32[16,256,128]{2,1,0:T(8,128)S(1)} %get-tuple-element.7, bf16[16,256,128]{2,1,0:T(8,128)(2,1)S(1)} %get-tuple-element.8), kind=kLoop, calls=%fused_computation | loop fusion | flops 1048576 | bytes 5242880 | tf_op jit(solution)/shard_map/add | solution.py:407

commit v5 on v4

--- a/solution.py
+++ b/solution.py
@@ -237,6 +237,8 @@
         one.start()
     for one in halos[2]:
         one.start()
+    for one in halos[3]:
+        one.start()
     for n in (4, 5, 6):
         mid_got[n].wait_recv()
     send_across((3, -3, 4))
@@ -248,8 +250,6 @@
     rows[r] = reduced.astype(BF16)
     rows_out = [copy(rows.at[r], rows.at[r], d_send.at[o], d_recv.at[o], mates[o]) for o in range(3)]
     for one in rows_out:
-        one.start()
-    for one in halos[3]:
         one.start()
 
     reach = [(ha0, ha1, 6, 18), (hb0, hb1, 4, 22), (hc0, hc1, 2, 26), (hd0, hd1, 0, 30)]
@@ -319,6 +319,8 @@
         down = dot(upl_t[q], value).reshape(8, RANK, HALF)
         lfield[pl.ds(8 * q, 8)] = lfield[pl.ds(8 * q, 8)] + down
 
+    forward(2)
+
     def product_step(k, _):
         for i in range(4):
             inner_leaf, outer_leaf = 4 + 4 * k + i, 12 * k + i
@@ -328,7 +330,6 @@
 
     lax.fori_loop(0, 2, product_step, 0)
 
-    forward(2)
     forward(3)
     near_phase(2)
     near_phase(3)

time: 43.1 us -> 42.5 us (0.986)
  no operation moved by 1% of the time
where the time goes in v5:
time: 42.5 us; the launch traced here: 42.4 us
  Pallas kernels  40.8 us (96%)
  other arithmetic  1.53 us (4%)
    pallas_call x1, Pallas kernels, shards(): pl.pallas_call(kernel, out_shape=(jax.ShapeDtypeStruct((OWN, LEAF, HALF),...  40.8 us
    add x1, other arithmetic, shards(): return (near + take.astype(F32)).reshape(OWN * LEAF, HALF)  1.53 us

profile of v5, /device:TPU:1, one launch (start us, length us, event | category | flops | bytes accessed | tf_op | source)
XLA Modules:
  0.0 42.4 jit_solution(13655300183588195100)
XLA Ops:
  0.0 40.8 %h2_product.1 = (f32[16,256,128]{2,1,0:T(8,128)S(1)}, bf16[16,256,128]{2,1,0:T(8,128)(2,1)S(1)}) custom-call(bf16[16,256,128]{2,1,0:T(8,128)(2,1)} %bitcast.4, bf16[16,4,256,256]{3,2,1,0:T(8,128)(2,1)} %tiles.1, s32[8,16]{1,0:T(8,128)} %bitcast.5, s32[16]{0:T(128)} %near_count_in.1, bf16[16,64,256]{2,1,0:T(8,128)(2,1)} %basis.1, ...), custom_call_target="tpu_custom_call" | custom-call | tf_op jit(solution)/shard_map/h2_product/pallas_call | solution.py:358
  40.8 1.5 %convert_add_fusion = f32[16,256,128]{2,1,0:T(8,128)} fusion(f32[16,256,128]{2,1,0:T(8,128)S(1)} %get-tuple-element.7, bf16[16,256,128]{2,1,0:T(8,128)(2,1)S(1)} %get-tuple-element.8), kind=kLoop, calls=%fused_computation | loop fusion | flops 1048576 | bytes 5242880 | tf_op jit(solution)/shard_map/add | solution.py:408
